TPU v7x, 256 devices: a whole 4x4x8 slice. The times are simulated.
256 devices in a mesh: dp: 4 (over x_hi, core), ctx: 64 (over x_lo, y, z).
Axes of the slice: x: 4 (x_hi: 2, x_lo: 2; x = x_hi * 2 + x_lo), y: 4, z: 8, core: 2. Of those that a mesh axis runs over, the one named last changes fastest.
Arguments:
- residual: bfloat16 [4096, 16, 1024], P('ctx', 'dp'), may hold values from -10 to 10
- projections: bfloat16 [4096, 16, 3072], P('ctx', 'dp'), may hold values from -8 to 8
- out_weight: bfloat16 [1024, 1024], replicated, may hold values from -0.1875 to 0.1875
- gain_one: float32 [1024], replicated, may hold values from 0.1 to 1.9
- up_weight: bfloat16 [1024, 2048], replicated, may hold values from -0.1875 to 0.1875
- conv_kernel: float32 [31, 1024], replicated, may hold values from -1 to 1
- gain_two: float32 [1024], replicated, may hold values from 0.1 to 1.9
- down_weight: bfloat16 [1024, 1024], replicated, may hold values from -0.1875 to 0.1875
- lengths: int32 [16], P('dp'), may hold values from 1024 to 4096, as said below
- out_grad: bfloat16 [4096, 16, 1024], P('ctx', 'dp'), may hold values from -0.0625 to 0.0625
Outputs:
- block_out: bfloat16 [4096, 16, 1024], P('ctx', 'dp')
- up_grad: float32 [2048, 1024], P(('dp', 'ctx'))
- down_grad: float32 [1024, 1024], P(('dp', 'ctx'))
- kernel_grad: float32 [1024, 31], P(('dp', 'ctx'))
- gain_one_grad: float32 [1024], P(('dp', 'ctx'))
- gain_two_grad: float32 [1024], P(('dp', 'ctx'))
Inputs may be any that keep to these rules, and one draw needn't show every extreme that they name: `lengths`: utterance 0 has all 4096 frames valid.
All inputs are finite; a program needn't handle non-finite values.
Results may differ from a plain program's by a relative error of at most 0.02.
Values may be sent and summed in bfloat16 or wider, within the bound.
A program may use at most 128 MiB of HBM per device.

v0:
```python
import math

import jax
import jax.numpy as jnp
from jax import lax
from jax.sharding import PartitionSpec as P

HEADS = 16


EPSILON = 1e-05


def extended(x, sides, width):
    for axis, dim in sides:
        size, length = (lax.axis_size(axis), x.shape[dim])
        up = [(i, (i + 1) % size) for i in range(size - 1)]
        down = [(j, i) for i, j in up]
        last = lax.slice_in_dim(x, length - width, length, axis=dim)
        leading = lax.slice_in_dim(x, 0, width, axis=dim)
        before = lax.ppermute(last, axis, up)
        after = lax.ppermute(leading, axis, down)
        x = jnp.concatenate([before, x, after], axis=dim)
    return x


def normalize(values):
    center = values - jnp.mean(values, axis=-1, keepdims=True)
    inverse = lax.rsqrt(jnp.mean(center * center, axis=-1, keepdims=True) + EPSILON)
    return (center * inverse, inverse)


def attend(pieces):
    packed_four, marks_three = pieces
    length = packed_four.shape[0]
    count = packed_four.shape[2]
    triple = packed_four.shape[3]
    packed = packed_four.reshape(length, count, triple)
    key_marks = marks_three.reshape(length, count)
    head_size = triple // 3
    query_rows = packed[:, :, :head_size]
    key_rows = packed[:, :, head_size : 2 * head_size]
    value_rows = packed[:, :, 2 * head_size :]
    allowed = jnp.transpose(key_marks > 0)
    block_span = math.gcd(length, 512)
    blocks = query_rows.reshape(length // block_span, block_span, count, head_size)
    score_scale = head_size ** (-0.5)

    def one_block(query_block):
        scores = (
            jnp.einsum("qmd,kmd->mqk", query_block, key_rows, preferred_element_type=jnp.float32)
            * score_scale
        )
        scores = jnp.where(allowed[:, None, :], scores, -jnp.inf)
        highest = jnp.max(scores, axis=-1, keepdims=True)
        raised = jnp.exp(scores - highest)
        weights_bf = (raised / jnp.sum(raised, axis=-1, keepdims=True)).astype(jnp.bfloat16)
        return jnp.einsum(
            "mqk,kmd->qmd", weights_bf, value_rows, preferred_element_type=jnp.float32
        ).astype(jnp.bfloat16)

    return lax.map(one_block, blocks).reshape(length, 1, count, head_size)


def on_device(
    residual,
    projections,
    out_weight,
    gain_one,
    up_weight,
    conv_kernel,
    gain_two,
    down_weight,
    lengths,
    out_grad,
):
    frames, utter_count, model_width = residual.shape
    head_count = HEADS
    head_size = model_width // head_count
    kernel_len = conv_kernel.shape[0]
    half_width = (kernel_len - 1) // 2
    row_count = frames * utter_count
    ctx_count = lax.axis_size("ctx")
    per_device = utter_count * head_count // ctx_count
    first_frame = lax.axis_index("ctx") * frames
    positions = first_frame + jnp.arange(frames, dtype=jnp.int32)
    valid = (positions[:, None] < lengths[None, :]).astype(jnp.bfloat16)
    key_marks = jnp.broadcast_to(valid[:, :, None], (frames, utter_count, head_count)).reshape(
        frames, ctx_count, per_device
    )
    packed = projections.reshape(frames, ctx_count, per_device, 3 * head_size)
    by_head = attend(
        (
            lax.all_to_all(packed, "ctx", split_axis=1, concat_axis=0, tiled=True),
            lax.all_to_all(key_marks, "ctx", split_axis=1, concat_axis=0, tiled=True),
        )
    )
    by_frame = lax.all_to_all(by_head, "ctx", split_axis=0, concat_axis=1, tiled=True)
    context = by_frame.reshape(row_count, model_width)
    hidden = residual.reshape(row_count, model_width).astype(jnp.float32) + jnp.dot(
        context, out_weight, preferred_element_type=jnp.float32
    )
    normed_one, inverse_one = normalize(hidden)
    scaled_one = (normed_one * gain_one).astype(jnp.bfloat16)
    lifted = jnp.dot(scaled_one, up_weight, preferred_element_type=jnp.float32)
    linear_part = lifted[:, :model_width]
    gate_part = jax.nn.sigmoid(lifted[:, model_width:])
    row_mask = valid.reshape(row_count, 1).astype(jnp.float32)
    glu_out = (linear_part * gate_part * row_mask).astype(jnp.bfloat16)
    glu_rimmed = extended(
        glu_out.reshape(frames, utter_count, model_width), (("ctx", 0),), half_width
    )
    glu_wide = glu_rimmed.astype(jnp.float32)
    conv_out = jnp.zeros((frames, utter_count, model_width), jnp.float32)
    for offset in range(kernel_len):
        conv_out = conv_out + conv_kernel[offset] * glu_wide[offset : offset + frames]
    normed_two, inverse_two = normalize(conv_out.reshape(row_count, model_width))
    pre_act = normed_two * gain_two
    gate_two = jax.nn.sigmoid(pre_act)
    activated = (pre_act * gate_two).astype(jnp.bfloat16)
    block_out = (
        hidden + jnp.dot(activated, down_weight, preferred_element_type=jnp.float32)
    ).astype(jnp.bfloat16)
    block_out = block_out.reshape(frames, utter_count, model_width)
    cotangent = (out_grad * valid[:, :, None]).reshape(row_count, model_width)
    down_grad = jnp.einsum("ro,ri->oi", cotangent, activated, preferred_element_type=jnp.float32)
    act_grad = lax.dot_general(
        cotangent, down_weight, (((1,), (1,)), ((), ())), preferred_element_type=jnp.float32
    )
    pre_grad = act_grad * gate_two * (1.0 + pre_act * (1.0 - gate_two))
    gain_two_grad = jnp.sum(pre_grad * normed_two, axis=0)
    scaled_grad = pre_grad * gain_two
    conv_grad = inverse_two * (
        scaled_grad
        - jnp.mean(scaled_grad, axis=-1, keepdims=True)
        - normed_two * jnp.mean(scaled_grad * normed_two, axis=-1, keepdims=True)
    )
    conv_grad = conv_grad.astype(jnp.bfloat16).reshape(frames, utter_count, model_width)
    conv_rimmed = extended(conv_grad, (("ctx", 0),), half_width)
    conv_wide = conv_rimmed.astype(jnp.float32)
    conv_local = conv_wide[half_width : half_width + frames]
    kernel_cols = []
    glu_grad = jnp.zeros((frames, utter_count, model_width), jnp.float32)
    for offset in range(kernel_len):
        kernel_cols.append(jnp.sum(conv_local * glu_wide[offset : offset + frames], axis=(0, 1)))
        start_row = 2 * half_width - offset
        glu_grad = glu_grad + conv_kernel[offset] * conv_wide[start_row : start_row + frames]
    kernel_grad = jnp.stack(kernel_cols, axis=1)
    glu_grad = glu_grad.reshape(row_count, model_width) * row_mask
    linear_grad = glu_grad * gate_part
    gate_grad = glu_grad * linear_part * gate_part * (1.0 - gate_part)
    lifted_grad = jnp.concatenate([linear_grad, gate_grad], axis=1).astype(jnp.bfloat16)
    up_grad = jnp.einsum("rj,ri->ji", lifted_grad, scaled_one, preferred_element_type=jnp.float32)
    input_grad = lax.dot_general(
        lifted_grad, up_weight, (((1,), (1,)), ((), ())), preferred_element_type=jnp.float32
    )
    gain_one_grad = jnp.sum(input_grad * normed_one, axis=0)
    summed = (
        lax.psum_scatter(up_grad, ("dp", "ctx"), scatter_dimension=0, tiled=True),
        lax.psum_scatter(down_grad, ("dp", "ctx"), scatter_dimension=0, tiled=True),
        lax.psum_scatter(kernel_grad, ("dp", "ctx"), scatter_dimension=0, tiled=True),
        lax.psum_scatter(gain_one_grad, ("dp", "ctx"), scatter_dimension=0, tiled=True),
        lax.psum_scatter(gain_two_grad, ("dp", "ctx"), scatter_dimension=0, tiled=True),
    )
    return (block_out, summed[0], summed[1], summed[2], summed[3], summed[4])


def solution(mesh):
    in_specs = (
        P("ctx", "dp", None),
        P("ctx", "dp", None),
        P(),
        P(),
        P(),
        P(),
        P(),
        P(),
        P("dp"),
        P("ctx", "dp", None),
    )
    out_specs = (
        P("ctx", "dp", None),
        P(("dp", "ctx"), None),
        P(("dp", "ctx"), None),
        P(("dp", "ctx"), None),
        P(("dp", "ctx")),
        P(("dp", "ctx")),
    )
    return jax.shard_map(
        on_device, mesh=mesh, in_specs=in_specs, out_specs=out_specs, check_vma=False
    )
```

profile of v0, /device:TPU:32, one launch (start us, length us, event | category | flops | bytes accessed | tf_op | source)
XLA Modules:
  0.0 1849.1 jit_solution(12558975090910986204)
XLA Ops:
  8.7 12.7 all-to-all-start
  21.4 4.6 reshape.262
  26.0 4.1 copy.116
  30.9 11.2 all-to-all-start.1
  42.4 50.6 %all-to-all-done.1 = bf16[64,64,1,192]{3,0,2,1:T(8,128)(2,1)} async-done(((bf16[64,64,1,192]{3,0,2,1:T(8,128)(2,1)}), bf16[64,64,1,192]{3,0,2,1:T(8,128)(2,1)}, u32[]{:S(2)}, u32[]{:S(2)}) %all-to-all-start.1) | async-done | bytes 1572896 | tf_op jit(solution)/shard_map/all_to_all | solution.py:94
  93.0 3.6 fusion.67
  101.6 60.6 %while.10 = (s32[]{:T(128)}, bf16[8,512,1,64]{1,3,2,0:T(8,128)(2,1)}, pred[4096,1]{0,1:T(4,128)(4,1)S(1)}, bf16[8,512,1,64]{1,3,2,0:T(8,128)(2,1)}, bf16[4096,1,...) while((s32[]{:T(128)}, bf16[8,512,1,64]{1,3,2,0:T(8,128)(2,1)}, ...), condition=%wide.region_3.4_spmd, body=%wide.region_0.3_spmd.sunk | while | flops 562068480 | bytes 28474480 | solution.py:62
  106.1 3.1 fusion.87
  151.5 3.1 fusion.87
  163.7 3.2 reshape.277
  167.4 23.4 %reduce.7 = bf16[4096,64]{1,0:T(8,128)(2,1)S(1)} reduce(bf16[4096,1,1,64]{3,2,1,0:T(2,128)(2,1)} %reshape.277, bf16[]{:T(256)} %broadcast.177), dimensions={1,2}, to_apply=%reshape.277.reduce_sub_computation | reduce | bytes 1048578 | tf_op jit(solution)/shard_map/reshape | solution.py:62
  192.4 5.7 all-to-all-start.2
  203.5 11.9 all-to-all-done.2
  215.4 3.6 reshape.282
  219.0 5.2 copy.122
  251.7 5.5 fusion.66
  262.2 3.3 multiply_reduce_fusion
  274.3 4.4 convolution_bitcast_fusion
  290.2 20.9 %fusion.17 = f32[64,4,1024]{2,0,1:T(8,128)S(1)} fusion(f32[94,4,1024]{2,0,1:T(8,128)} %copy-done.3, f32[1024]{0:T(1024)S(1)} %bitcast.194, f32[1024]{0:T(1024)S(1)} %bitcast.196, f32[1024]{0:T(1024)S(1)} %bitcast.138, f32[1024]{0:T(1024)S(1)} %bitcast.140, f32[1024]{0:T(1024)S(1)} %bitcast.142, f32[1024]{0:T(1024)S(1)} %bitcast.144, f32[1024]{0:T(1024)S(1)} %bitcast.146, ...), kind=kLoop, calls=%fused_computation.26 | loop fusion | flops 15990784 | bytes 33681408 | tf_op jit(solution)/shard_map/add | solution.py:147
  318.7 4.6 fusion.50
  329.0 3.9 fusion.16
  332.8 83.3 %all-reduce.4 = (f32[1024]{0:T(1024)S(1)}, f32[1024]{0:T(1024)S(1)}) all-reduce(f32[1024]{0:T(1024)S(1)} %fusion.16, f32[1024]{0:T(1024)S(1)} %copy-done.80), channel_id=5, replica_groups=mesh['dp'=4,'ctx'=64] {'dp','ctx'}, use_global_device_ids=true, to_apply=%region_45.46.clone | all-reduce | flops 2048 | bytes 16384
  417.3 143.8 %all-reduce.8.cloned.1.call-done = (f32[1024,1024]{1,0:T(8,128)}, f32[1024,31]{0,1:T(8,128)}) async-done(((f32[1024,1024]{1,0:T(8,128)}, f32[1024,31]{0,1:T(8,128)}), (f32[1024,1024]{1,0:T(8,128)}, f32[1024,31]{0,1:T(8,128)})) %all-reduce.8.cloned.1.call-update) | async-done | bytes 4321296
  563.9 1278.1 %reduce-scatter.3.cloned.1.call-done = f32[8,1024]{1,0:T(8,128)} async-done(((f32[2048,1024]{1,0:T(8,128)}), f32[8,1024]{1,0:T(8,128)}) %reduce-scatter.3.cloned.1.call-update) | async-done | bytes 32784 | tf_op jit(solution)/shard_map/reduce_scatter | solution.py:159
  (294 shorter events, 139.7 us)
Async XLA Ops:
  7.2 255.0 %copy-start = (bf16[1024,1024]{1,0:T(8,128)(2,1)S(1)}, bf16[1024,1024]{1,0:T(8,128)(2,1)}, u32[]{:S(2)}) copy-start(bf16[1024,1024]{1,0:T(8,128)(2,1)} %param.19) | copy-start | bytes 6291460
  8.7 22.2 %all-to-all-start = ((bf16[64,64,1]{0,2,1:T(2,128)(2,1)}), bf16[64,64,1]{0,2,1:T(2,128)(2,1)S(1)}, u32[]{:S(2)}, u32[]{:S(2)}) async-start(bf16[64,64,1]{0,2,1:T(2,128)(2,1)} %copy.113), calls=%async_computation | async-start | bytes 65536 | tf_op jit(solution)/shard_map/all_to_all | solution.py:95
  30.9 62.1 %all-to-all-start.1 = ((bf16[64,64,1,192]{3,0,2,1:T(8,128)(2,1)}), bf16[64,64,1,192]{3,0,2,1:T(8,128)(2,1)}, u32[]{:S(2)}, u32[]{:S(2)}) async-start(bf16[64,64,1,192]{3,0,2,1:T(8,128)(2,1)} %copy.116), calls=%async_computation.1 | async-start | bytes 4194304 | tf_op jit(solution)/shard_map/all_to_all | solution.py:94
  192.4 23.0 %all-to-all-start.2 = ((bf16[64,2,2048]{2,1,0:T(2,128)(2,1)}), bf16[64,2,2048]{2,1,0:T(2,128)(2,1)S(1)}, u32[]{:S(2)}, u32[]{:S(2)}) async-start(bf16[64,2,2048]{2,1,0:T(2,128)(2,1)} %reshape.281), calls=%async_computation.2 | async-start | bytes 1048576 | tf_op jit(solution)/shard_map/all_to_all | solution.py:98
  198.0 4.8 copy-start.13
  198.0 363.0 %all-reduce.8.cloned.1.call-start = ((), (), s32[]{:S(2)}) async-start(), calls=%async_computation.5 | async-start | bytes 8650752
  200.5 36.0 %copy-start.65 = (f32[256]{0:T(256)}, f32[256]{0:T(256)S(1)}, u32[]{:S(2)}) copy-start(f32[256]{0:T(256)S(1)} %reshape.275) | copy-start | bytes 3076
  201.9 17.1 copy-start.11
  239.8 11.4 collective-permute-start
  243.4 7.7 collective-permute-start.1
  247.6 3.8 copy-start.40
  247.7 3.8 copy-start.42
  247.7 3.8 copy-start.44
  247.7 3.8 copy-start.46
  247.7 3.8 copy-start.48
  247.7 3.8 copy-start.50
  251.4 5.8 copy-start.1
  259.2 6.3 copy-start.69
  259.4 6.1 copy-start.70
  267.5 14.6 collective-permute-start.2
  271.2 10.9 collective-permute-start.3
  289.6 1552.4 %reduce-scatter.3.cloned.1.call-start = ((), (), s32[]{:S(2)}) async-start(), calls=%async_computation.4 | async-start | bytes 8421376 | tf_op jit(solution)/shard_map/reduce_scatter | solution.py:159
  311.1 4.3 copy-start.66
  329.0 3.9 copy-start.80
  (74 other events, 150.4 us)
Sparse Core Ops, SparseCore 0:
  289.7 271.3 all-reduce.7
  564.3 1277.6 reduce-scatter.2
where the time goes:
time: 1860 us; the launch traced here: 1850 us
  waiting for transfers between devices  1490 us (80%)
  blocking collectives  83.3 us (4%)
  local copies, waits for them, and re-layouts  78.8 us (4%)
  other arithmetic  78 us (4%)
  matrix products  66.2 us (4%)
  starting transfers between devices  41.9 us (2%)
    reduce_scatter x1, waiting for transfers between devices, on_device(): lax.psum_scatter(up_grad, ('dp', 'ctx'), scatter_dimension=0, tiled=True)  1280 us
    unnamed x3, waiting for transfers between devices  144 us
    unnamed x1, blocking collectives  83.3 us
    all_to_all x1, waiting for transfers between devices, on_device(): lax.all_to_all(packed, 'ctx', split_axis=1, concat_axis=0, tiled=True)  50.6 us
  transfers between devices with their start and end apart: 9, of which 5 were waited for; matrix products, arithmetic and copies ran while one was open for 4% of the time, Pallas kernels for 0%

commit v1 on v0

--- a/solution.py
+++ b/solution.py
@@ -1,14 +1,441 @@
-import math
+import functools
 
 import jax
 import jax.numpy as jnp
 from jax import lax
+from jax.experimental import pallas as pl
+from jax.experimental.pallas import tpu as pltpu
 from jax.sharding import PartitionSpec as P
 
 HEADS = 16
-
-
 EPSILON = 1e-05
+LOG2E = 1.4426950408889634
+MESH = pl.DeviceIdType.MESH
+BF16 = jnp.bfloat16
+F32 = jnp.float32
+
+PART_Z = (0, 384)
+PART_Y = (384, 640)
+PART_X = (1024, 640)
+CHUNK = 1664
+
+
+def lane_ids(shape):
+    return lax.broadcasted_iota(jnp.int32, shape, len(shape) - 1)
+
+
+def attend_kernel(
+    proj, lengths, out,
+    pbuf, rows32, kv_send, q_send, kv_recv, q_recv, o_send, o_recv, keys, values,
+    load_sem, kv_ssem, q_ssem, o_ssem, kv_rsem, q_rsem, o_rsem,
+):
+    dp = lax.axis_index("dp")
+    me = lax.axis_index("ctx")
+    group, pair = me // 8, me // 2
+    load = pltpu.make_async_copy(proj, pbuf, load_sem)
+    load.start()
+    barrier = pltpu.get_barrier_semaphore()
+
+    def greet(step, carry):
+        pl.semaphore_signal(
+            barrier, inc=1, device_id=(dp, lax.rem(me + step, 64)), device_id_type=MESH
+        )
+        return carry
+
+    lax.fori_loop(1, 64, greet, 0)
+    load.wait()
+
+    def widen(step, carry):
+        both = jnp.concatenate([pbuf[step * 2 + i].astype(F32) for i in range(2)], axis=0)
+        for tile in range(24):
+            rows32[tile, pl.ds(pl.multiple_of(step * 8, 8), 8), :] = both[
+                :, tile * 128 : tile * 128 + 128
+            ]
+        return carry
+
+    lax.fori_loop(0, 32, widen, 0)
+    pl.semaphore_wait(barrier, 63)
+
+    def push(src, dst, ssem, rsem, target):
+        @pl.when(target != me)
+        def _():
+            pltpu.make_async_remote_copy(
+                src_ref=src, dst_ref=dst, send_sem=ssem, recv_sem=rsem,
+                device_id=(dp, target), device_id_type=MESH,
+            ).start()
+
+        @pl.when(target == me)
+        def _():
+            pltpu.make_async_copy(src, dst, rsem).start()
+
+    low = lane_ids((64, 128)) < 64
+    low32 = lane_ids((32, 128)) < 64
+
+    def pack(step, carry):
+        which = lax.rem(pair + step, 32)
+        utt, duo = which // 8, lax.rem(which, 8)
+        rows = pl.ds(utt, 64, stride=4)
+        first, second, third = [rows32[duo * 3 + i, rows, :] for i in range(3)]
+        first_t, second_t = pltpu.roll(first, 64, 1), pltpu.roll(second, 64, 1)
+        kv_send[which * 2] = jnp.where(low, first_t, second_t).astype(BF16)
+        kv_send[which * 2 + 1] = third.astype(BF16)
+        q_send[which * 2] = jnp.where(low32, first[:32], first_t[32:]).astype(BF16)
+        q_send[which * 2 + 1] = jnp.where(low32, second_t[:32], second[32:]).astype(BF16)
+        for side in range(2):
+            target = which * 2 + side
+            push(kv_send.at[target], kv_recv.at[me], kv_ssem, kv_rsem.at[group], target)
+        return carry
+
+    lax.fori_loop(0, 32, pack, 0)
+
+    def ask(step, carry):
+        which = lax.rem(pair + step, 32)
+        for side in range(2):
+            target = which * 2 + side
+            push(q_send.at[target], q_recv.at[me], q_ssem, q_rsem.at[group], target)
+        return carry
+
+    lax.fori_loop(0, 32, ask, 0)
+
+    length = lengths[me // 16]
+
+    def take_keys(step, carry):
+        src = lax.rem(group - step + 8, 8)
+        eight = pl.ds(pl.multiple_of(src * 8, 8), 8)
+        pltpu.make_async_copy(kv_recv.at[eight], kv_recv.at[eight], kv_rsem.at[src]).wait()
+        kv = kv_recv[eight].reshape(512, 128).astype(F32)
+        lane = lane_ids((512, 128))
+        base = pl.multiple_of(src * 512, 512)
+        frame = base + lax.broadcasted_iota(jnp.int32, (512, 128), 0)
+        block = pl.ds(base, 512)
+        keys[block, :128] = jnp.where(lane < 64, kv, pltpu.roll(kv, 64, 1)).astype(BF16)
+        keys[block, 128:] = jnp.where((lane == 0) & (frame >= length), -30000.0, 0.0).astype(BF16)
+        values[block, :] = jnp.where(lane < 64, 1.0, kv).astype(BF16)
+        return carry
+
+    lax.fori_loop(0, 8, take_keys, 0)
+
+    def attend(step, carry):
+        src = lax.rem(group - step + 8, 8)
+        eight = pl.ds(pl.multiple_of(src * 8, 8), 8)
+        pltpu.make_async_copy(q_recv.at[eight], q_recv.at[eight], q_rsem.at[src]).wait()
+        half = lane_ids((256, 128))
+        query = q_recv[eight].reshape(256, 128).astype(F32) * (0.125 * LOG2E)
+        high = query.astype(BF16).astype(F32)
+        rest = query - high
+        one = jnp.where(half == 0, 1.0, 0.0)
+        early = jnp.where(half < 64, high, pltpu.roll(rest, 64, 1))
+        late = jnp.where(half < 64, pltpu.roll(high, 64, 1), rest)
+        query = jnp.concatenate(
+            [jnp.concatenate([early, one], axis=1), jnp.concatenate([late, one], axis=1)], axis=0
+        ).astype(BF16)
+
+        def scores(c):
+            return lax.dot_general(
+                query, keys[c * 512 : (c + 1) * 512, :], (((1,), (1,)), ((), ())),
+                preferred_element_type=F32,
+            )
+
+        highest = jnp.full((512, 1), -1e30, F32)
+        total = jnp.zeros((512, 128), F32)
+        now = scores(0)
+        for c in range(8):
+            later = scores(c + 1) if c < 7 else None
+            top = jnp.maximum(highest, jnp.max(now, axis=1, keepdims=True))
+            probs = jnp.exp2(now - top).astype(BF16)
+            total = total * jnp.exp2(highest - top) + jnp.dot(
+                probs, values[c * 512 : (c + 1) * 512, :], preferred_element_type=F32
+            )
+            highest, now = top, later
+        normed = total / pltpu.roll(total, 64, 1)
+        context = jnp.where(half < 64, pltpu.roll(normed[:256], 64, 1), normed[256:])
+        o_send[eight] = context.astype(BF16).reshape(8, 32, 128)
+
+        def reply(item, inner):
+            target = src * 8 + item
+            push(o_send.at[target], o_recv.at[me], o_ssem, o_rsem.at[group], target)
+            return inner
+
+        lax.fori_loop(0, 8, reply, 0)
+        return carry
+
+    lax.fori_loop(0, 8, attend, 0)
+
+    def gather(step, carry):
+        src = lax.rem(group + step, 8)
+        eight = pl.ds(pl.multiple_of(src * 8, 8), 8)
+        pltpu.make_async_copy(o_recv.at[eight], o_recv.at[eight], o_rsem.at[src]).wait()
+        for i in range(4):
+            which = src * 4 + i
+            utt, duo = which // 8, lax.rem(which, 8)
+            left = o_recv[which * 2].astype(F32)
+            right = o_recv[which * 2 + 1].astype(F32)
+            upper = jnp.where(low32, left, pltpu.roll(right, 64, 1))
+            lower = jnp.where(low32, pltpu.roll(left, 64, 1), right)
+            rows32[duo, pl.ds(utt, 64, stride=4), :] = jnp.concatenate([upper, lower], axis=0)
+        return carry
+
+    lax.fori_loop(0, 8, gather, 0)
+    for tile in range(8):
+        out[:, tile * 128 : tile * 128 + 128] = rows32[tile].astype(BF16)
+    for buf, sem in ((kv_send, kv_ssem), (q_send, q_ssem), (o_send, o_ssem)):
+        sent = buf.at[pl.ds(0, 63)]
+        pltpu.make_async_copy(sent, sent, sem).wait()
+
+
+def attend(projections, lengths):
+    dma = pltpu.SemaphoreType.DMA
+    return pl.pallas_call(
+        attend_kernel,
+        out_shape=jax.ShapeDtypeStruct((256, 1024), BF16),
+        in_specs=[
+            pl.BlockSpec(memory_space=pl.ANY),
+            pl.BlockSpec(memory_space=pltpu.SMEM),
+        ],
+        out_specs=pl.BlockSpec(memory_space=pltpu.VMEM),
+        scratch_shapes=[
+            pltpu.VMEM((64, 4, 3072), BF16),
+            pltpu.VMEM((24, 256, 128), F32),
+            pltpu.VMEM((64, 64, 128), BF16),
+            pltpu.VMEM((64, 32, 128), BF16),
+            pltpu.VMEM((64, 64, 128), BF16),
+            pltpu.VMEM((64, 32, 128), BF16),
+            pltpu.VMEM((64, 32, 128), BF16),
+            pltpu.VMEM((64, 32, 128), BF16),
+            pltpu.VMEM((4096, 256), BF16),
+            pltpu.VMEM((4096, 128), BF16),
+            dma, dma, dma, dma,
+            dma((8,)), dma((8,)), dma((8,)),
+        ],
+        compiler_params=pltpu.CompilerParams(
+            collective_id=1, has_side_effects=True, vmem_limit_bytes=48 << 20
+        ),
+        name="exchange_attend",
+    )(projections, lengths)
+
+
+def sum_kernel(
+    grads, out,
+    mine, other, y_recv, y_sum, yx_recv, yx_sum, yxz_recv,
+    x_recv, x_sum, xy_recv, xy_sum, xyz_recv,
+    z_recv, z_sum, zx_recv, zx_sum, zxy_recv,
+    lsem, ssem, rsem,
+):
+    dp, ctx = lax.axis_index("dp"), lax.axis_index("ctx")
+    x_hi, core = dp // 2, lax.rem(dp, 2)
+    x_lo, y, z = ctx // 32, lax.rem(ctx // 8, 4), lax.rem(ctx, 8)
+    x = x_hi * 2 + x_lo
+    sibling = (x_hi * 2 + 1 - core, ctx)
+
+    def along_x(k):
+        to = lax.rem(x + k, 4)
+        return (to // 2) * 2 + core, lax.rem(to, 2) * 32 + y * 8 + z
+
+    def along_y(k):
+        return dp, x_lo * 32 + lax.rem(y + k, 4) * 8 + z
+
+    def along_z(k):
+        return dp, x_lo * 32 + y * 8 + lax.rem(z + k, 8)
+
+    locals_ = []
+    for i, (start, width) in enumerate((PART_Y, PART_X, PART_Z)):
+        part = pl.ds(start, width)
+        copy = pltpu.make_async_copy(
+            grads.at[:, core, :, :, :, :, part], mine.at[:, :, :, :, :, part], lsem.at[i]
+        )
+        copy.start()
+        locals_.append(copy)
+
+    barrier = pltpu.get_barrier_semaphore()
+    peers = [sibling] + [along_x(k) for k in (1, 2, 3)] + [along_y(k) for k in (1, 2, 3)]
+    peers += [along_z(k) for k in range(1, 8)]
+    for peer in peers:
+        pl.semaphore_signal(barrier, inc=1, device_id=peer, device_id_type=MESH)
+    pl.semaphore_wait(barrier, len(peers))
+
+    started = []
+
+    def send(src, dst, peer):
+        index = len(started)
+        copy = pltpu.make_async_remote_copy(
+            src_ref=src, dst_ref=dst, send_sem=ssem.at[index], recv_sem=rsem.at[index],
+            device_id=peer, device_id_type=MESH,
+        )
+        copy.start()
+        started.append(copy)
+        return copy
+
+    halves = []
+    for start, width in (PART_Y, PART_X, PART_Z):
+        part = pl.ds(start, width)
+        halves.append(
+            send(
+                grads.at[:, 1 - core, :, :, :, :, part],
+                other.at[:, :, :, :, :, part],
+                sibling,
+            )
+        )
+
+    def join(i, part):
+        start, width = part
+        locals_[i].wait()
+        halves[i].wait_recv()
+        cols = pl.ds(start, width)
+
+        def body(step, carry):
+            a, b, c = step // 8, lax.rem(step // 4, 2), lax.rem(step, 4)
+            mine[a, b, c, :, :, cols] = (
+                mine[a, b, c, :, :, cols].astype(F32) + other[a, b, c, :, :, cols].astype(F32)
+            ).astype(BF16)
+            return carry
+
+        lax.fori_loop(0, 16, body, 0)
+
+    def cols_of(part):
+        return pl.ds(part[0], part[1])
+
+    def split(k):
+        to = lax.rem(x + k, 4)
+        return to // 2, lax.rem(to, 2)
+
+    join(0, PART_Y)
+    y_one = [
+        send(
+            mine.at[:, :, lax.rem(y + k, 4), :, :, cols_of(PART_Y)], y_recv.at[k - 1], along_y(k)
+        )
+        for k in (1, 2, 3)
+    ]
+    join(1, PART_X)
+    x_one = []
+    for k in (1, 2, 3):
+        hi, lo = split(k)
+        x_one.append(send(mine.at[hi, lo, :, :, :, cols_of(PART_X)], x_recv.at[k - 1], along_x(k)))
+    join(2, PART_Z)
+    z_one = [
+        send(
+            mine.at[:, :, :, lax.rem(z + k, 8), :, cols_of(PART_Z)], z_recv.at[k - 1], along_z(k)
+        )
+        for k in range(1, 8)
+    ]
+
+    def wait_all(copies):
+        for copy in copies:
+            copy.wait_recv()
+
+    wait_all(y_one)
+
+    def y_body(step, carry):
+        a, b = step // 2, lax.rem(step, 2)
+        acc = mine[a, b, y, :, :, cols_of(PART_Y)].astype(F32)
+        for k in range(3):
+            acc = acc + y_recv[k, a, b].astype(F32)
+        y_sum[a, b] = acc.astype(BF16)
+        return carry
+
+    lax.fori_loop(0, 4, y_body, 0)
+    yx = []
+    for k in (1, 2, 3):
+        hi, lo = split(k)
+        yx.append(send(y_sum.at[hi, lo], yx_recv.at[k - 1], along_x(k)))
+
+    wait_all(x_one)
+
+    def x_body(step, carry):
+        acc = mine[x_hi, x_lo, step, :, :, cols_of(PART_X)].astype(F32)
+        for k in range(3):
+            acc = acc + x_recv[k, step].astype(F32)
+        x_sum[step] = acc.astype(BF16)
+        return carry
+
+    lax.fori_loop(0, 4, x_body, 0)
+    xy = [
+        send(x_sum.at[lax.rem(y + k, 4)], xy_recv.at[k - 1], along_y(k)) for k in (1, 2, 3)
+    ]
+
+    wait_all(z_one)
+
+    def z_body(step, carry):
+        a, b = step // 2, lax.rem(step, 2)
+        acc = mine[a, b, :, z, :, cols_of(PART_Z)].astype(F32)
+        for k in range(7):
+            acc = acc + z_recv[k, a, b].astype(F32)
+        z_sum[a, b] = acc.astype(BF16)
+        return carry
+
+    lax.fori_loop(0, 4, z_body, 0)
+    zx = []
+    for k in (1, 2, 3):
+        hi, lo = split(k)
+        zx.append(send(z_sum.at[hi, lo], zx_recv.at[k - 1], along_x(k)))
+
+    wait_all(yx)
+    acc = y_sum[x_hi, x_lo].astype(F32)
+    for k in range(3):
+        acc = acc + yx_recv[k].astype(F32)
+    yx_sum[...] = acc.astype(BF16)
+    yxz = [
+        send(yx_sum.at[lax.rem(z + k, 8)], yxz_recv.at[k - 1], along_z(k)) for k in range(1, 8)
+    ]
+
+    wait_all(xy)
+    acc = x_sum[y].astype(F32)
+    for k in range(3):
+        acc = acc + xy_recv[k].astype(F32)
+    xy_sum[...] = acc.astype(BF16)
+    xyz = [
+        send(xy_sum.at[lax.rem(z + k, 8)], xyz_recv.at[k - 1], along_z(k)) for k in range(1, 8)
+    ]
+
+    wait_all(zx)
+    acc = z_sum[x_hi, x_lo].astype(F32)
+    for k in range(3):
+        acc = acc + zx_recv[k].astype(F32)
+    zx_sum[...] = acc.astype(BF16)
+    zxy = [
+        send(zx_sum.at[lax.rem(y + k, 4)], zxy_recv.at[k - 1], along_y(k)) for k in (1, 2, 3)
+    ]
+
+    for copies, own, received, count, part in (
+        (yxz, yx_sum.at[z], yxz_recv, 7, PART_Y),
+        (xyz, xy_sum.at[z], xyz_recv, 7, PART_X),
+        (zxy, zx_sum.at[y], zxy_recv, 3, PART_Z),
+    ):
+        wait_all(copies)
+        acc = own[...].astype(F32)
+        for k in range(count):
+            acc = acc + received[k].astype(F32)
+        out[:, cols_of(part)] = acc
+    for copy in started:
+        copy.wait_send()
+
+
+def sum_everywhere(grads):
+    dma = pltpu.SemaphoreType.DMA
+    wide, narrow = PART_Y[1], PART_Z[1]
+
+    def vmem(*shape):
+        return pltpu.VMEM(shape, BF16)
+
+    return pl.pallas_call(
+        sum_kernel,
+        out_shape=jax.ShapeDtypeStruct((8, CHUNK), F32),
+        in_specs=[pl.BlockSpec(memory_space=pl.ANY)],
+        out_specs=pl.BlockSpec(memory_space=pltpu.VMEM),
+        scratch_shapes=[
+            vmem(2, 2, 4, 8, 8, CHUNK), vmem(2, 2, 4, 8, 8, CHUNK),
+            vmem(3, 2, 2, 8, 8, wide), vmem(2, 2, 8, 8, wide),
+            vmem(3, 8, 8, wide), vmem(8, 8, wide), vmem(7, 8, wide),
+            vmem(3, 4, 8, 8, wide), vmem(4, 8, 8, wide),
+            vmem(3, 8, 8, wide), vmem(8, 8, wide), vmem(7, 8, wide),
+            vmem(7, 2, 2, 4, 8, narrow), vmem(2, 2, 4, 8, narrow),
+            vmem(3, 4, 8, narrow), vmem(4, 8, narrow), vmem(3, 8, narrow),
+            dma((3,)), dma((48,)), dma((48,)),
+        ],
+        compiler_params=pltpu.CompilerParams(
+            collective_id=2, has_side_effects=True, vmem_limit_bytes=48 << 20
+        ),
+        name="sum_everywhere",
+    )(grads.reshape(2, 2, 2, 4, 8, 8, CHUNK))
 
 
 def extended(x, sides, width):
@@ -28,38 +455,6 @@
     center = values - jnp.mean(values, axis=-1, keepdims=True)
     inverse = lax.rsqrt(jnp.mean(center * center, axis=-1, keepdims=True) + EPSILON)
     return (center * inverse, inverse)
-
-
-def attend(pieces):
-    packed_four, marks_three = pieces
-    length = packed_four.shape[0]
-    count = packed_four.shape[2]
-    triple = packed_four.shape[3]
-    packed = packed_four.reshape(length, count, triple)
-    key_marks = marks_three.reshape(length, count)
-    head_size = triple // 3
-    query_rows = packed[:, :, :head_size]
-    key_rows = packed[:, :, head_size : 2 * head_size]
-    value_rows = packed[:, :, 2 * head_size :]
-    allowed = jnp.transpose(key_marks > 0)
-    block_span = math.gcd(length, 512)
-    blocks = query_rows.reshape(length // block_span, block_span, count, head_size)
-    score_scale = head_size ** (-0.5)
-
-    def one_block(query_block):
-        scores = (
-            jnp.einsum("qmd,kmd->mqk", query_block, key_rows, preferred_element_type=jnp.float32)
-            * score_scale
-        )
-        scores = jnp.where(allowed[:, None, :], scores, -jnp.inf)
-        highest = jnp.max(scores, axis=-1, keepdims=True)
-        raised = jnp.exp(scores - highest)
-        weights_bf = (raised / jnp.sum(raised, axis=-1, keepdims=True)).astype(jnp.bfloat16)
-        return jnp.einsum(
-            "mqk,kmd->qmd", weights_bf, value_rows, preferred_element_type=jnp.float32
-        ).astype(jnp.bfloat16)
-
-    return lax.map(one_block, blocks).reshape(length, 1, count, head_size)
 
 
 def on_device(
@@ -75,28 +470,13 @@
     out_grad,
 ):
     frames, utter_count, model_width = residual.shape
-    head_count = HEADS
-    head_size = model_width // head_count
     kernel_len = conv_kernel.shape[0]
     half_width = (kernel_len - 1) // 2
     row_count = frames * utter_count
-    ctx_count = lax.axis_size("ctx")
-    per_device = utter_count * head_count // ctx_count
     first_frame = lax.axis_index("ctx") * frames
     positions = first_frame + jnp.arange(frames, dtype=jnp.int32)
     valid = (positions[:, None] < lengths[None, :]).astype(jnp.bfloat16)
-    key_marks = jnp.broadcast_to(valid[:, :, None], (frames, utter_count, head_count)).reshape(
-        frames, ctx_count, per_device
-    )
-    packed = projections.reshape(frames, ctx_count, per_device, 3 * head_size)
-    by_head = attend(
-        (
-            lax.all_to_all(packed, "ctx", split_axis=1, concat_axis=0, tiled=True),
-            lax.all_to_all(key_marks, "ctx", split_axis=1, concat_axis=0, tiled=True),
-        )
-    )
-    by_frame = lax.all_to_all(by_head, "ctx", split_axis=0, concat_axis=1, tiled=True)
-    context = by_frame.reshape(row_count, model_width)
+    context = attend(projections, lengths)
     hidden = residual.reshape(row_count, model_width).astype(jnp.float32) + jnp.dot(
         context, out_weight, preferred_element_type=jnp.float32
     )
@@ -145,7 +525,6 @@
         kernel_cols.append(jnp.sum(conv_local * glu_wide[offset : offset + frames], axis=(0, 1)))
         start_row = 2 * half_width - offset
         glu_grad = glu_grad + conv_kernel[offset] * conv_wide[start_row : start_row + frames]
-    kernel_grad = jnp.stack(kernel_cols, axis=1)
     glu_grad = glu_grad.reshape(row_count, model_width) * row_mask
     linear_grad = glu_grad * gate_part
     gate_grad = glu_grad * linear_part * gate_part * (1.0 - gate_part)
@@ -155,14 +534,24 @@
         lifted_grad, up_weight, (((1,), (1,)), ((), ())), preferred_element_type=jnp.float32
     )
     gain_one_grad = jnp.sum(input_grad * normed_one, axis=0)
-    summed = (
-        lax.psum_scatter(up_grad, ("dp", "ctx"), scatter_dimension=0, tiled=True),
-        lax.psum_scatter(down_grad, ("dp", "ctx"), scatter_dimension=0, tiled=True),
-        lax.psum_scatter(kernel_grad, ("dp", "ctx"), scatter_dimension=0, tiled=True),
-        lax.psum_scatter(gain_one_grad, ("dp", "ctx"), scatter_dimension=0, tiled=True),
-        lax.psum_scatter(gain_two_grad, ("dp", "ctx"), scatter_dimension=0, tiled=True),
-    )
-    return (block_out, summed[0], summed[1], summed[2], summed[3], summed[4])
+    small = jnp.stack(kernel_cols + [gain_one_grad, gain_two_grad], axis=1).reshape(256, 4, 33)
+    chunks = jnp.concatenate(
+        [
+            up_grad.astype(BF16).reshape(256, 8, 1024),
+            down_grad.astype(BF16).reshape(256, 4, 2, 512).transpose(0, 2, 1, 3).reshape(256, 8, 512),
+            jnp.pad(small.astype(BF16), ((0, 0), (0, 4), (0, 95))),
+        ],
+        axis=2,
+    )
+    total = sum_everywhere(chunks)
+    return (
+        block_out,
+        total[:, :1024],
+        total[:, 1024:1536].reshape(2, 4, 512).transpose(1, 0, 2).reshape(4, 1024),
+        total[:4, 1536:1567],
+        total[:4, 1567],
+        total[:4, 1568],
+    )
 
 
 def solution(mesh):

time: 1860 us -> 228 us (0.12)
  waiting for transfers between devices: 1490 us -> 0.01 us
  Pallas kernels: 0 us -> 117 us
  blocking collectives: 83.3 us -> 0 us
  other arithmetic: 78 us -> 26.2 us
  matrix products: 66.2 us -> 19.7 us
  local copies, waits for them, and re-layouts: 78.8 us -> 48.8 us
  starting transfers between devices: 41.9 us -> 12.1 us
    reduce_scatter x1 -> x0, waiting for transfers between devices: 1280 us -> none  [on_device(): lax.psum_scatter(up_grad, ('dp', 'ctx'), scatter_dimension=0, tiled=True)]
    unnamed x3 -> x0, waiting for transfers between devices: 144 us -> none
    pallas_call x0 -> x2, Pallas kernels: none -> 117 us  [the longest x1 73.8 us: attend(): pl.pallas_call(attend_kernel, out_shape=jax.ShapeDtypeStruct((256, 1024),...]
    unnamed x1 -> x0, blocking collectives: 83.3 us -> none
    all_to_all x3 -> x0, waiting for transfers between devices: 63.3 us -> none  [the longest x1 50.6 us: on_device(): lax.all_to_all(packed, 'ctx', split_axis=1, concat_axis=0, tiled=True)]
    dot_general x16 -> x0, matrix products: 42.8 us -> none  [the longest x8 25 us: one_block(): jnp.einsum('mqk,kmd->qmd', weights_bf, value_rows, preferred_element_type...]
    all_to_all x3 -> x0, starting transfers between devices: 29.5 us -> none  [the longest x1 12.7 us: on_device(): lax.all_to_all(key_marks, 'ctx', split_axis=1, concat_axis=0, tiled=True)]
    reshape x1 -> x0, other arithmetic: 23.4 us -> none  [attend(): return lax.map(one_block, blocks).reshape(length, 1, count, head_size)]
  transfers between devices with their start and end apart: 9 -> 4, of which waited for: 5 -> 0; matrix products, arithmetic and copies ran while one was open for 4% -> 12% of each run, Pallas kernels for 0% -> 0%
where the time goes in v1:
time: 228 us; the launch traced here: 226 us
  Pallas kernels  117 us (51%)
  local copies, waits for them, and re-layouts  48.8 us (21%)
  other arithmetic  26.2 us (11%)
  matrix products  19.7 us (9%)
  starting transfers between devices  12.1 us (5%)
  between operations  2.31 us (1%)
    pallas_call x1, Pallas kernels, attend(): pl.pallas_call(attend_kernel, out_shape=jax.ShapeDtypeStruct((256, 1024),...  73.8 us
    pallas_call x1, Pallas kernels, sum_everywhere(): pl.pallas_call(sum_kernel, out_shape=jax.ShapeDtypeStruct((8, CHUNK), F32...  42.9 us
    another operation x67, local copies, waits for them, and re-layouts, on_device(): jnp.stack(kernel_cols + [gain_one_grad, gain_two_grad], axis=1)  9.77 us
    reshape x2, local copies, waits for them, and re-layouts, on_device(): down_grad.astype(BF16).reshape(256, 4, 2, 512).transpose(0, 2, 1, 3)  8.46 us
    ppermute x2, starting transfers between devices, extended(): after = lax.ppermute(leading, axis, down)  6.57 us
    unnamed x203, local copies, waits for them, and re-layouts  6.15 us
    concatenate x1, other arithmetic, on_device(): jnp.concatenate([up_grad.astype(BF16).reshape(256, 8, 1024), down_grad.as...  6.09 us
    reduce_sum x1, other arithmetic, normalize(): center = values - jnp.mean(values, axis=-1, keepdims=True)  5.52 us
  transfers between devices with their start and end apart: 4, of which 0 were waited for; matrix products, arithmetic and copies ran while one was open for 12% of the time, Pallas kernels for 0%

profile of v1, /device:TPU:32, one launch (start us, length us, event | category | flops | bytes accessed | tf_op | source)
XLA Modules:
  0.0 225.7 jit_solution(12583930882238462573)
XLA Ops:
  3.7 73.8 %exchange_attend.1 = bf16[256,1024]{1,0:T(8,128)(2,1)S(1)} custom-call(bf16[64,4,3072]{2,1,0:T(4,128)(2,1)S(1)} %copy-done.1, s32[4]{0:T(128)S(1)} %copy-done.2), custom_call_target="tpu_custom_call" | custom-call | tf_op jit(solution)/shard_map/exchange_attend/pallas_call | solution.py:188
  78.6 2.8 %fusion.56 = (f32[256]{0:T(256)S(1)}, f32[256,1024]{1,0:T(8,128)S(1)}) fusion(f32[256,1024]{1,0:T(8,128)} %reshape.314, bf16[256,1024]{1,0:T(8,128)(2,1)S(1)} %exchange_attend.1, bf16[1024,1024]{1,0:T(8,128)(2,1)} %param.12), kind=kOutput, calls=%fused_computation.188 | convolution fusion | flops 537394944 | bytes 4719616 | tf_op jit(solution)/shard_map/dot_general | solution.py:480
  84.9 3.3 %collective-permute-start.1 = (bf16[15,4,1024]{2,0,1:T(8,128)(2,1)S(1)}, bf16[15,4,1024]{2,0,1:T(8,128)(2,1)S(1)}, u32[]{:S(2)}, u32[]{:S(2)}) collective-permute-start(bf16[15,4,1024]{2,0,1:T(8,128)(2,1)S(1)} %copy.42), channel_id=1, source_target_pairs={{1,0},{2,1},{3,2},{4,3},{5,4},{6,5},{7,6},{8,7},{9,8},{10,9},{11,1... | collective-permute-start | bytes 368648 | tf_op jit(solution)/shard_map/ppermute | solution.py:449
  89.0 2.7 %collective-permute-start = (bf16[15,4,1024]{2,0,1:T(8,128)(2,1)}, bf16[15,4,1024]{2,0,1:T(8,128)(2,1)S(1)}, u32[]{:S(2)}, u32[]{:S(2)}) collective-permute-start(bf16[15,4,1024]{2,0,1:T(8,128)(2,1)} %copy.41), channel_id=1, source_target_pairs={{0,1},{1,2},{2,3},{3,4},{4,5},{5,6},{6,7},{7,8},{8,9},{9,10},{10,1... | collective-permute-start | bytes 368648 | tf_op jit(solution)/shard_map/ppermute | solution.py:448
  91.9 2.0 fusion.54
  98.3 5.5 %fusion.51 = (f32[64,4]{0,1:T(4,128)S(1)}, f32[64,4,1024]{2,0,1:T(8,128)S(1)}) fusion(f32[94,4,1024]{2,0,1:T(8,128)S(1)} %maximum_convert_fusion, f32[1024]{0:T(1024)S(1)} %bitcast.109, f32[1024]{0:T(1024)S(1)} %bitcast.111, f32[1024]{0:T(1024)S(1)} %bitcast.53, f32[1024]{0:T(1024)S(1)} %bitcast.55, f32[1024]{0:T(1024)S(1)} %bitcast.57, ...), kind=kLoop, calls=%fused_computation.183 | loop fusion | flops 16252672 | bytes 33682432 | tf_op jit(solution)/shard_map/reduce_sum | solution.py:455
  104.3 1.7 copy.44
  106.3 2.6 %reshape.306 = f32[256,1024]{1,0:T(8,128)} reshape(f32[64,4,1024]{2,1,0:T(4,128)} %copy.44) | data formatting | bytes 2097152 | tf_op jit(solution)/shard_map/reshape | solution.py:497
  108.9 3.3 %fusion.1 = bf16[256,1024]{1,0:T(8,128)(2,1)} fusion(f32[256,1024]{1,0:T(8,128)} %copy-done.6, bf16[1024,1024]{1,0:T(8,128)(2,1)S(1)} %copy-done, f32[256,1024]{1,0:T(8,128)} %reshape.306, f32[1024]{0:T(1024)S(1)} %copy-done.77, f32[256]{0:T(256)S(1)} %rsqrt.22, f32[256]{0:T(256)S(1)} %div.33), kind=kOutput, calls=%fused_computation.9 | convolution fusion | flops 539492352 | bytes 4724736 | tf_op jit(solution)/shard_map/dot_general | solution.py:502
  112.2 1.8 multiply_reduce_fusion
  116.0 3.3 %collective-permute-start.3 = (bf16[15,4,1024]{2,0,1:T(8,128)(2,1)S(1)}, bf16[15,4,1024]{2,0,1:T(8,128)(2,1)S(1)}, u32[]{:S(2)}, u32[]{:S(2)}) collective-permute-start(bf16[15,4,1024]{2,0,1:T(8,128)(2,1)S(1)} %copy.48), channel_id=1, source_target_pairs={{1,0},{2,1},{3,2},{4,3},{5,4},{6,5},{7,6},{8,7},{9,8},{10,9},{11,1... | collective-permute-start | bytes 368648 | tf_op jit(solution)/shard_map/ppermute | solution.py:449
  119.3 2.8 %collective-permute-start.2 = (bf16[15,4,1024]{2,0,1:T(8,128)(2,1)}, bf16[15,4,1024]{2,0,1:T(8,128)(2,1)S(1)}, u32[]{:S(2)}, u32[]{:S(2)}) collective-permute-start(bf16[15,4,1024]{2,0,1:T(8,128)(2,1)} %copy.47), channel_id=1, source_target_pairs={{0,1},{1,2},{2,3},{3,4},{4,5},{5,6},{6,7},{7,8},{8,9},{9,10},{10,1... | collective-permute-start | bytes 368648 | tf_op jit(solution)/shard_map/ppermute | solution.py:448
  122.1 3.4 %bitcast_convert_fusion = bf16[1024,1024]{1,0:T(8,128)(2,1)} fusion(f32[64,4,1024]{2,0,1:T(8,128)S(1)} %get-tuple-element.43, bf16[64,4,1024]{2,1,0:T(4,128)(2,1)} %copy-done.10, f32[1024]{0:T(1024)} %param.16, f32[64,4]{0,1:T(4,128)} %copy-done.76, f32[64,4]{0,1:T(4,128)} %copy-done.72), kind=kOutput, calls=%fused_computation.1 | convolution fusion | flops 540016640 | bytes 3676160 | tf_op jit(solution)/shard_map/ro,ri->oi/dot_general | solution.py:506
  126.8 4.5 %reshape.311 = bf16[256,4,2,512]{3,2,1,0:T(2,128)(2,1)} reshape(bf16[1024,1024]{1,0:T(8,128)(2,1)} %bitcast_convert_fusion) | data formatting | bytes 4194304 | tf_op jit(solution)/shard_map/reshape | solution.py:541
  131.3 4.0 %copy.92 = bf16[256,4,2,512]{3,1,2,0:T(4,128)(2,1)} copy(bf16[256,4,2,512]{3,2,1,0:T(2,128)(2,1)} %reshape.311) | data formatting | bytes 4194304 | tf_op jit(solution)/shard_map/reshape | solution.py:541
  135.2 4.1 %concatenate.26 = bf16[2,2,2,4,8,8,512]{6,5,4,3,2,1,0:T(8,128)(2,1)} reshape(bf16[256,2,4,512]{3,2,1,0:T(4,128)(2,1)} %bitcast.48) | data formatting | bytes 4194304 | tf_op jit(solution)/shard_map/concatenate | solution.py:538
  146.0 1.8 multiply_reduce_fusion.1
  148.1 4.4 %fusion.3 = f32[64,4,1024]{2,0,1:T(8,128)S(1)} fusion(f32[94,4,1024]{2,0,1:T(8,128)S(1)} %maximum_convert_fusion.1, f32[1024]{0:T(1024)S(1)} %bitcast.110, f32[1024]{0:T(1024)S(1)} %bitcast.112, f32[1024]{0:T(1024)S(1)} %bitcast.54, f32[1024]{0:T(1024)S(1)} %bitcast.56, f32[1024]{0:T(1024)S(1)} %bitcast.58, f32[1024]{0:T(1024)S(1)} %bitcast.60, ...), kind=kLoop, calls=%fused_computation.12 | loop fusion | flops 15990784 | bytes 33681408 | tf_op jit(solution)/shard_map/add | solution.py:527
  152.5 1.7 copy.50
  155.8 2.0 multiply_convert_fusion.2
  157.9 3.5 %fusion.2 = bf16[1024]{0:T(1024)(128)(2,1)S(1)} fusion(bf16[1024,2048]{1,0:T(8,128)(2,1)} %param.14, f32[256,1024]{1,0:T(8,128)S(1)} %copy-done.7, bf16[256,1024]{1,0:T(8,128)(2,1)S(1)} %get-tuple-element.45, bf16[256,1024]{1,0:T(8,128)(2,1)S(1)} %get-tuple-element.44, f32[256]{0:T(256)S(1)} %copy-done.81, f32[256]{0:T(256)S(1)} %copy-done.79), kind=kOutput, calls=%fused_computation.10 | convolution fusion | flops 1076886528 | bytes 6295552 | tf_op jit(solution)/shard_map/dot_general | solution.py:533
  161.4 3.5 %convolution_convert_fusion = bf16[2048,1024]{1,0:T(8,128)(2,1)} fusion(bf16[256,1024]{1,0:T(8,128)(2,1)S(1)} %get-tuple-element.45, bf16[256,1024]{1,0:T(8,128)(2,1)S(1)} %get-tuple-element.44, f32[256,1024]{1,0:T(8,128)S(1)} %copy-done.7, f32[1024]{0:T(1024)S(1)} %copy-done.84, f32[256]{0:T(256)S(1)} %copy-done.81, f32[256]{0:T(256)S(1)} %copy-done.79), kind=kOutput, calls=%fused_computation.2 | convolution fusion | flops 1078984704 | bytes 6297600 | tf_op jit(solution)/shard_map/rj,ri->ji/dot_general | solution.py:532
  174.2 6.1 %pad_maximum_fusion.grads = bf16[2,2,2,4,8,8,1664]{6,5,4,3,2,1,0:T(8,128)(2,1)} fusion(bf16[2,2,2,4,8,8,128]{6,5,4,3,2,1,0:T(8,128)(2,1)S(1)} %bitcast.50, bf16[2,2,2,4,8,8,512]{6,5,4,3,2,1,0:T(8,128)(2,1)} %concatenate.26, bf16[2,2,2,4,8,8,1024]{6,5,4,3,2,1,0:T(8,128)(2,1)} %bitcast.49), kind=kLoop, calls=%fused_computation | loop fusion | flops 20447232 | bytes 13631488 | tf_op jit(solution)/shard_map/concatenate | solution.py:538
  180.2 42.9 %sum_everywhere.1 = f32[8,1664]{1,0:T(8,128)S(1)} custom-call(bf16[2,2,2,4,8,8,1664]{6,5,4,3,2,1,0:T(8,128)(2,1)} %pad_maximum_fusion.grads), custom_call_target="tpu_custom_call" | custom-call | tf_op jit(solution)/shard_map/sum_everywhere/pallas_call | solution.py:419
  (321 shorter events, 36.1 us)
Async XLA Ops:
  0.6 108.2 %copy-start = (bf16[1024,1024]{1,0:T(8,128)(2,1)S(1)}, bf16[1024,1024]{1,0:T(8,128)(2,1)}, u32[]{:S(2)}) copy-start(bf16[1024,1024]{1,0:T(8,128)(2,1)} %param.17) | copy-start | bytes 6291460
  3.7 79.4 %copy-start.73 = (f32[256]{0:T(256)}, f32[256]{0:T(256)S(1)}, u32[]{:S(2)}) copy-start(f32[256]{0:T(256)S(1)} %reshape.316) | copy-start | bytes 3076
  3.7 73.8 %copy-start.11 = (bf16[64,4,1024]{2,1,0:T(4,128)(2,1)S(1)}, bf16[64,4,1024]{2,1,0:T(4,128)(2,1)}, u32[]{:S(2)}) copy-start(bf16[64,4,1024]{2,1,0:T(4,128)(2,1)} %param.10) | copy-start | bytes 1572868
  84.9 12.9 %collective-permute-start.1 = (bf16[15,4,1024]{2,0,1:T(8,128)(2,1)S(1)}, bf16[15,4,1024]{2,0,1:T(8,128)(2,1)S(1)}, u32[]{:S(2)}, u32[]{:S(2)}) collective-permute-start(bf16[15,4,1024]{2,0,1:T(8,128)(2,1)S(1)} %copy.42), channel_id=1, source_target_pairs={{1,0},{2,1},{3,2},{4,3},{5,4},{6,5},{7,6},{8,7},{9,8},{10,9},{11,1... | collective-permute-start | bytes 368648 | tf_op jit(solution)/shard_map/ppermute | solution.py:449
  89.0 8.8 %collective-permute-start = (bf16[15,4,1024]{2,0,1:T(8,128)(2,1)}, bf16[15,4,1024]{2,0,1:T(8,128)(2,1)S(1)}, u32[]{:S(2)}, u32[]{:S(2)}) collective-permute-start(bf16[15,4,1024]{2,0,1:T(8,128)(2,1)} %copy.41), channel_id=1, source_target_pairs={{0,1},{1,2},{2,3},{3,4},{4,5},{5,6},{6,7},{7,8},{8,9},{9,10},{10,1... | collective-permute-start | bytes 368648 | tf_op jit(solution)/shard_map/ppermute | solution.py:448
  97.7 6.1 %copy-start.48 = (f32[1,1024]{1,0:T(1,128)}, f32[1,1024]{1,0:T(1,128)S(1)}, u32[]{:S(2)}) copy-start(f32[1,1024]{1,0:T(1,128)S(1)} %get-tuple-element.73) | copy-start | bytes 12292
  97.7 6.1 %copy-start.50 = (f32[1,1024]{1,0:T(1,128)}, f32[1,1024]{1,0:T(1,128)S(1)}, u32[]{:S(2)}) copy-start(f32[1,1024]{1,0:T(1,128)S(1)} %get-tuple-element.74) | copy-start | bytes 12292
  97.7 6.1 %copy-start.52 = (f32[1,1024]{1,0:T(1,128)}, f32[1,1024]{1,0:T(1,128)S(1)}, u32[]{:S(2)}) copy-start(f32[1,1024]{1,0:T(1,128)S(1)} %get-tuple-element.75) | copy-start | bytes 12292
  97.7 6.1 %copy-start.54 = (f32[1,1024]{1,0:T(1,128)}, f32[1,1024]{1,0:T(1,128)S(1)}, u32[]{:S(2)}) copy-start(f32[1,1024]{1,0:T(1,128)S(1)} %get-tuple-element.76) | copy-start | bytes 12292
  97.7 6.1 %copy-start.56 = (f32[1,1024]{1,0:T(1,128)}, f32[1,1024]{1,0:T(1,128)S(1)}, u32[]{:S(2)}) copy-start(f32[1,1024]{1,0:T(1,128)S(1)} %get-tuple-element.77) | copy-start | bytes 12292
  97.7 6.1 %copy-start.58 = (f32[1,1024]{1,0:T(1,128)}, f32[1,1024]{1,0:T(1,128)S(1)}, u32[]{:S(2)}) copy-start(f32[1,1024]{1,0:T(1,128)S(1)} %get-tuple-element.78) | copy-start | bytes 12292
  97.7 6.1 %copy-start.60 = (f32[1,1024]{1,0:T(1,128)}, f32[1,1024]{1,0:T(1,128)S(1)}, u32[]{:S(2)}) copy-start(f32[1,1024]{1,0:T(1,128)S(1)} %get-tuple-element.79) | copy-start | bytes 12292
  97.7 6.1 %copy-start.62 = (f32[1,1024]{1,0:T(1,128)}, f32[1,1024]{1,0:T(1,128)S(1)}, u32[]{:S(2)}) copy-start(f32[1,1024]{1,0:T(1,128)S(1)} %get-tuple-element.80) | copy-start | bytes 12292
  97.8 6.1 %copy-start.64 = (f32[1,1024]{1,0:T(1,128)}, f32[1,1024]{1,0:T(1,128)S(1)}, u32[]{:S(2)}) copy-start(f32[1,1024]{1,0:T(1,128)S(1)} %get-tuple-element.81) | copy-start | bytes 12292
  97.8 6.1 %copy-start.66 = (f32[1,1024]{1,0:T(1,128)}, f32[1,1024]{1,0:T(1,128)S(1)}, u32[]{:S(2)}) copy-start(f32[1,1024]{1,0:T(1,128)S(1)} %get-tuple-element.82) | copy-start | bytes 12292
  97.8 6.1 %copy-start.68 = (f32[1,1024]{1,0:T(1,128)}, f32[1,1024]{1,0:T(1,128)S(1)}, u32[]{:S(2)}) copy-start(f32[1,1024]{1,0:T(1,128)S(1)} %get-tuple-element.83) | copy-start | bytes 12292
  97.8 6.1 %copy-start.70 = (f32[1,1024]{1,0:T(1,128)}, f32[1,1024]{1,0:T(1,128)S(1)}, u32[]{:S(2)}) copy-start(f32[1,1024]{1,0:T(1,128)S(1)} %get-tuple-element.84) | copy-start | bytes 12292
  98.1 5.9 %copy-start.3 = (f32[94,4,1024]{2,0,1:T(8,128)}, f32[94,4,1024]{2,0,1:T(8,128)S(1)}, u32[]{:S(2)}) copy-start(f32[94,4,1024]{2,0,1:T(8,128)S(1)} %maximum_convert_fusion) | copy-start | bytes 4620292
  104.3 4.6 %copy-start.77 = (f32[1024]{0:T(1024)S(1)}, f32[1024]{0:T(1024)}, u32[]{:S(2)}) copy-start(f32[1024]{0:T(1024)} %param.16) | copy-start | bytes 12292
  106.0 6.2 %copy-start.76 = (f32[64,4]{0,1:T(4,128)}, f32[64,4]{0,1:T(4,128)S(1)}, u32[]{:S(2)}) copy-start(f32[64,4]{0,1:T(4,128)S(1)} %add_rsqrt_fusion) | copy-start | bytes 3076
  116.0 25.9 %collective-permute-start.3 = (bf16[15,4,1024]{2,0,1:T(8,128)(2,1)S(1)}, bf16[15,4,1024]{2,0,1:T(8,128)(2,1)S(1)}, u32[]{:S(2)}, u32[]{:S(2)}) collective-permute-start(bf16[15,4,1024]{2,0,1:T(8,128)(2,1)S(1)} %copy.48), channel_id=1, source_target_pairs={{1,0},{2,1},{3,2},{4,3},{5,4},{6,5},{7,6},{8,7},{9,8},{10,9},{11,1... | collective-permute-start | bytes 368648 | tf_op jit(solution)/shard_map/ppermute | solution.py:449
  119.3 22.7 %collective-permute-start.2 = (bf16[15,4,1024]{2,0,1:T(8,128)(2,1)}, bf16[15,4,1024]{2,0,1:T(8,128)(2,1)S(1)}, u32[]{:S(2)}, u32[]{:S(2)}) collective-permute-start(bf16[15,4,1024]{2,0,1:T(8,128)(2,1)} %copy.47), channel_id=1, source_target_pairs={{0,1},{1,2},{2,3},{3,4},{4,5},{5,6},{6,7},{7,8},{8,9},{9,10},{10,1... | collective-permute-start | bytes 368648 | tf_op jit(solution)/shard_map/ppermute | solution.py:448
  135.2 4.1 %copy-start.13 = (bf16[256,1024]{1,0:T(8,128)(2,1)S(1)}, bf16[256,1024]{1,0:T(8,128)(2,1)}, u32[]{:S(2)}) copy-start(bf16[256,1024]{1,0:T(8,128)(2,1)} %fusion.1) | copy-start | bytes 1572868
  165.6 8.2 %copy-start.75 = (bf16[256,4,1]{0,1,2:T(4,128)(2,1)S(1)}, bf16[256,4,1]{0,1,2:T(4,128)(2,1)}, u32[]{:S(2)}) copy-start(bf16[256,4,1]{0,1,2:T(4,128)(2,1)} %copy.85) | copy-start | bytes 6148
  (65 other events, 137.9 us)

commit v2 on v1

--- a/solution.py
+++ b/solution.py
@@ -214,56 +214,16 @@
     )(projections, lengths)
 
 
-def sum_kernel(
-    grads, out,
-    mine, other, y_recv, y_sum, yx_recv, yx_sum, yxz_recv,
+def sum_phase(
+    where, send, grads, out,
+    other, y_recv, y_sum, yx_recv, yx_sum, yxz_recv,
     x_recv, x_sum, xy_recv, xy_sum, xyz_recv,
     z_recv, z_sum, zx_recv, zx_sum, zxy_recv,
-    lsem, ssem, rsem,
 ):
-    dp, ctx = lax.axis_index("dp"), lax.axis_index("ctx")
-    x_hi, core = dp // 2, lax.rem(dp, 2)
-    x_lo, y, z = ctx // 32, lax.rem(ctx // 8, 4), lax.rem(ctx, 8)
+    x_hi, x_lo, core, y, z = where.x_hi, where.x_lo, where.core, where.y, where.z
     x = x_hi * 2 + x_lo
-    sibling = (x_hi * 2 + 1 - core, ctx)
-
-    def along_x(k):
-        to = lax.rem(x + k, 4)
-        return (to // 2) * 2 + core, lax.rem(to, 2) * 32 + y * 8 + z
-
-    def along_y(k):
-        return dp, x_lo * 32 + lax.rem(y + k, 4) * 8 + z
-
-    def along_z(k):
-        return dp, x_lo * 32 + y * 8 + lax.rem(z + k, 8)
-
-    locals_ = []
-    for i, (start, width) in enumerate((PART_Y, PART_X, PART_Z)):
-        part = pl.ds(start, width)
-        copy = pltpu.make_async_copy(
-            grads.at[:, core, :, :, :, :, part], mine.at[:, :, :, :, :, part], lsem.at[i]
-        )
-        copy.start()
-        locals_.append(copy)
-
-    barrier = pltpu.get_barrier_semaphore()
-    peers = [sibling] + [along_x(k) for k in (1, 2, 3)] + [along_y(k) for k in (1, 2, 3)]
-    peers += [along_z(k) for k in range(1, 8)]
-    for peer in peers:
-        pl.semaphore_signal(barrier, inc=1, device_id=peer, device_id_type=MESH)
-    pl.semaphore_wait(barrier, len(peers))
-
-    started = []
-
-    def send(src, dst, peer):
-        index = len(started)
-        copy = pltpu.make_async_remote_copy(
-            src_ref=src, dst_ref=dst, send_sem=ssem.at[index], recv_sem=rsem.at[index],
-            device_id=peer, device_id_type=MESH,
-        )
-        copy.start()
-        started.append(copy)
-        return copy
+    along_x, along_y, along_z = where.along_x, where.along_y, where.along_z
+    mine = grads.at[:, core]
 
     halves = []
     for start, width in (PART_Y, PART_X, PART_Z):
@@ -272,13 +232,12 @@
             send(
                 grads.at[:, 1 - core, :, :, :, :, part],
                 other.at[:, :, :, :, :, part],
-                sibling,
+                where.sibling,
             )
         )
 
     def join(i, part):
         start, width = part
-        locals_[i].wait()
         halves[i].wait_recv()
         cols = pl.ds(start, width)
 
@@ -405,147 +364,362 @@
         for k in range(count):
             acc = acc + received[k].astype(F32)
         out[:, cols_of(part)] = acc
+
+
+class Place:
+    def __init__(self):
+        dp, ctx = lax.axis_index("dp"), lax.axis_index("ctx")
+        self.dp, self.ctx = dp, ctx
+        self.x_hi, self.core = dp // 2, lax.rem(dp, 2)
+        self.x_lo, self.y, self.z = ctx // 32, lax.rem(ctx // 8, 4), lax.rem(ctx, 8)
+        self.sibling = (self.x_hi * 2 + 1 - self.core, ctx)
+
+    def along_x(self, k):
+        to = lax.rem(self.x_hi * 2 + self.x_lo + k, 4)
+        return (to // 2) * 2 + self.core, lax.rem(to, 2) * 32 + self.y * 8 + self.z
+
+    def along_y(self, k):
+        return self.dp, self.x_lo * 32 + lax.rem(self.y + k, 4) * 8 + self.z
+
+    def along_z(self, k):
+        return self.dp, self.x_lo * 32 + self.y * 8 + lax.rem(self.z + k, 8)
+
+
+def rowwise(body):
+    def step(i, carry):
+        body(pl.ds(pl.multiple_of(i * 16, 16), 16))
+        return carry
+
+    lax.fori_loop(0, 16, step, 0)
+
+
+def colwise(body, count=4):
+    def step(i, carry):
+        body(i, pl.ds(pl.multiple_of(i * 256, 256), 256))
+        return carry
+
+    lax.fori_loop(0, count, step, 0)
+
+
+def dot(a, b):
+    return jnp.dot(a, b, preferred_element_type=F32)
+
+
+def dot_t(a, b):
+    return lax.dot_general(a, b, (((1,), (1,)), ((), ())), preferred_element_type=F32)
+
+
+def t_dot(a, b):
+    return lax.dot_general(a, b, (((0,), (0,)), ((), ())), preferred_element_type=F32)
+
+
+def moments(values):
+    center = values - jnp.mean(values, axis=-1, keepdims=True)
+    inverse = lax.rsqrt(jnp.mean(center * center, axis=-1, keepdims=True) + EPSILON)
+    return center * inverse, inverse
+
+
+def sigmoid(x):
+    return 1.0 / (1.0 + jnp.exp(-x))
+
+
+def four_later(src, dst):
+    def step(i, carry):
+        base = pl.multiple_of(i * 8, 8)
+        dst[pl.ds(base, 8), :] = jnp.concatenate(
+            [src[pl.ds(base, 8), :][4:], src[pl.ds(base + 8, 8), :][:4]], axis=0
+        )
+        return carry
+
+    lax.fori_loop(0, 47, step, 0)
+
+
+def block_kernel(
+    context, residual, out_grad, lengths, gain_one, gain_two, taps,
+    out_w_hbm, up_w_hbm, down_w_hbm,
+    block_out, total_out,
+    out_w, up_w, down_w, mask, hidden, normed_one, scaled_one, linear, gate, glu,
+    glu_even, glu_odd, grad_even, grad_odd, conv, normed_two, inverse_two, activated,
+    cotangent, act_grad, conv_grad, lifted_grad, before, after, tap_sums, sums, turned, grads,
+    *rest,
+):
+    sum_scratch, (wsem, ssem, rsem) = rest[:-3], rest[-3:]
+    where = Place()
+    ctx = where.ctx
+    weights = []
+    for i, (src, dst) in enumerate(((out_w_hbm, out_w), (up_w_hbm, up_w), (down_w_hbm, down_w))):
+        copy = pltpu.make_async_copy(src, dst, wsem.at[i])
+        copy.start()
+        weights.append(copy)
+
+    barrier = pltpu.get_barrier_semaphore()
+    axis_peers = [where.along_x(k) for k in (1, 2, 3)] + [where.along_y(k) for k in (1, 2, 3)]
+    axis_peers += [where.along_z(k) for k in range(1, 8)]
+    left, right = (where.dp, lax.rem(ctx + 63, 64)), (where.dp, lax.rem(ctx + 1, 64))
+    peers = [where.sibling, left, right] + axis_peers
+    for peer in peers:
+        pl.semaphore_signal(barrier, inc=1, device_id=peer, device_id_type=MESH)
+
+    started = []
+
+    def send(src, dst, peer):
+        index = len(started)
+        copy = pltpu.make_async_remote_copy(
+            src_ref=src, dst_ref=dst, send_sem=ssem.at[index], recv_sem=rsem.at[index],
+            device_id=peer, device_id_type=MESH,
+        )
+        copy.start()
+        started.append(copy)
+        return copy
+
+    row = lax.broadcasted_iota(jnp.int32, (256, 128), 0)
+    utt = lax.rem(row, 4)
+    limit = jnp.where(
+        utt < 2,
+        jnp.where(utt == 0, lengths[0], lengths[1]),
+        jnp.where(utt == 2, lengths[2], lengths[3]),
+    )
+    mask[...] = jnp.where(ctx * 64 + row // 4 < limit, 1.0, 0.0)
+
+    weights[0].wait()
+
+    def project(i, cols):
+        hidden[:, cols] = residual[:, cols].astype(F32) + dot(context[...], out_w[:, cols])
+
+    colwise(project)
+
+    def first_norm(rows):
+        normed, _ = moments(hidden[rows, :])
+        normed_one[rows, :] = normed
+        scaled_one[rows, :] = (normed * gain_one[...]).astype(BF16)
+        keep = jnp.tile(mask[rows, :], (1, 8))
+        cotangent[rows, :] = (out_grad[rows, :].astype(F32) * keep).astype(BF16)
+
+    rowwise(first_norm)
+    weights[1].wait()
+
+    def lift(i, cols):
+        lin = dot(scaled_one[...], up_w[:, cols])
+        gated = sigmoid(dot(scaled_one[...], up_w[:, pl.ds(pl.multiple_of(i * 256 + 1024, 256), 256)]))
+        keep = jnp.tile(mask[...], (1, 2))
+        product = (lin * gated * keep).astype(BF16)
+        linear[:, cols] = lin
+        gate[:, cols] = gated
+        glu[:, cols] = product
+        glu_even[pl.ds(64, 256), cols] = product.astype(F32)
+
+    colwise(lift)
+    pl.semaphore_wait(barrier, len(peers))
+
+    def swap_rims(src, dst):
+        up = send(src.at[pl.ds(192, 64)], before.at[dst], right)
+        down = send(src.at[pl.ds(0, 64)], after.at[dst], left)
+        return up, down
+
+    def take_rims(copies, slot, dst):
+        for copy in copies:
+            copy.wait_recv()
+        dst[pl.ds(0, 64), :] = jnp.where(ctx > 0, before[slot].astype(F32), 0.0)
+        dst[pl.ds(320, 64), :] = jnp.where(ctx < 63, after[slot].astype(F32), 0.0)
+
+    rims = swap_rims(glu, 0)
+    weights[2].wait()
+
+    def lift_back(i, cols):
+        act_grad[:, cols] = dot_t(cotangent[...], down_w[cols, :])
+
+    colwise(lift_back)
+    take_rims(rims, 0, glu_even)
+    four_later(glu_even, glu_odd)
+
+    def tiles(body):
+        def step(i, carry):
+            tile, block = i // 4, lax.rem(i, 4)
+            body(pl.multiple_of(block * 64, 64), pl.ds(pl.multiple_of(tile * 128, 128), 128))
+            return carry
+
+        lax.fori_loop(0, 32, step, 0)
+
+    def shifted(even, odd, base, ahead, cols):
+        if ahead % 2 == 0:
+            return even[pl.ds(base + ahead * 4, 64), cols]
+        return odd[pl.ds(base + ahead * 4 - 4, 64), cols]
+
+    def convolve(base, cols):
+        acc = jnp.zeros((64, 128), F32)
+        for j in range(31):
+            acc = acc + taps[j : j + 1, cols] * shifted(glu_even, glu_odd, base, j + 1, cols)
+        conv[pl.ds(base, 64), cols] = acc
+
+    tiles(convolve)
+    sums[...] = jnp.zeros_like(sums)
+
+    def second_norm(rows):
+        normed, inverse = moments(conv[rows, :])
+        pre = normed * gain_two[...]
+        s = sigmoid(pre)
+        activated[rows, :] = (pre * s).astype(BF16)
+        back = act_grad[rows, :] * s * (1.0 + pre * (1.0 - s))
+        weighted = back * normed
+        sums[0] += weighted[:8] + weighted[8:]
+        q = back * gain_two[...]
+        mean_q = jnp.mean(q, axis=-1, keepdims=True)
+        mean_qn = jnp.mean(q * normed, axis=-1, keepdims=True)
+        result = (inverse * (q - mean_q - normed * mean_qn)).astype(BF16)
+        conv_grad[rows, :] = result
+        grad_even[pl.ds(rows.start + 64, 16), :] = result.astype(F32)
+
+    rowwise(second_norm)
+    rims = swap_rims(conv_grad, 1)
+
+    def finish(i, cols):
+        block_out[:, cols] = (hidden[:, cols] + dot(activated[...], down_w[:, cols])).astype(BF16)
+
+    colwise(finish)
+
+    upper = lax.broadcasted_iota(jnp.int32, (32, 8, 512), 1) < 4
+
+    def down_tile(i, cols):
+        tile = t_dot(cotangent[:, cols], activated[...]).reshape(32, 8, 1024)
+        first, second = tile[:, :, :512], tile[:, :, 512:]
+        even = jnp.where(upper, first, pltpu.roll(second, 4, 1)).astype(BF16)
+        odd = jnp.where(upper, pltpu.roll(first, 4, 1), second).astype(BF16)
+        for n in range(32):
+            x_lo, y, z = n // 16, (n // 4) % 4, 2 * (n % 4)
+            grads[i // 2, lax.rem(i, 2), x_lo, y, z, :, pl.ds(1024, 512)] = even[n]
+            grads[i // 2, lax.rem(i, 2), x_lo, y, z + 1, :, pl.ds(1024, 512)] = odd[n]
+
+    colwise(down_tile)
+
+    def tap_step(i, carry):
+        cols = pl.ds(pl.multiple_of(i * 128, 128), 128)
+        for block in range(4):
+            local = grad_even[pl.ds(64 + block * 64, 64), cols]
+            for j in range(31):
+                product = local * shifted(glu_even, glu_odd, block * 64, j + 1, cols)
+                part = jnp.sum(product.reshape(8, 8, 128), axis=0)
+                if block == 0:
+                    tap_sums[j, :, cols] = part
+                else:
+                    tap_sums[j, :, cols] += part
+        return carry
+
+    lax.fori_loop(0, 8, tap_step, 0)
+    take_rims(rims, 1, grad_even)
+    four_later(grad_even, grad_odd)
+
+    def convolve_back(base, cols):
+        acc = jnp.zeros((64, 128), F32)
+        for j in range(31):
+            acc = acc + taps[j : j + 1, cols] * shifted(grad_even, grad_odd, base, 31 - j, cols)
+        rows = pl.ds(base, 64)
+        acc = acc * mask[rows, :]
+        g = gate[rows, cols]
+        acc_g = acc * g
+        lifted_grad[rows, cols] = acc_g.astype(BF16)
+        other_cols = pl.ds(pl.multiple_of(cols.start + 1024, 128), 128)
+        lifted_grad[rows, other_cols] = (acc_g * linear[rows, cols] * (1.0 - g)).astype(BF16)
+
+    tiles(convolve_back)
+
+    def up_tile(i, cols):
+        tile = t_dot(lifted_grad[:, cols], scaled_one[...]).reshape(4, 8, 8, 1024).astype(BF16)
+        grads[i // 4, lax.rem(i // 2, 2), lax.rem(i, 2), :, :, :, pl.ds(0, 1024)] = tile
+
+    colwise(up_tile, 8)
+
+    def input_tile(i, cols):
+        grad = dot_t(lifted_grad[...], up_w[cols, :])
+        product = grad * normed_one[:, cols]
+        sums[1, :, cols] = jnp.sum(product.reshape(32, 8, 256), axis=0)
+
+    colwise(input_tile)
+
+    rows_33 = [jnp.sum(tap_sums[j], axis=0, keepdims=True) for j in range(31)]
+    rows_33 += [jnp.sum(sums[1], axis=0, keepdims=True), jnp.sum(sums[0], axis=0, keepdims=True)]
+    small = jnp.concatenate(rows_33 + [jnp.zeros((128 - 33, 1024), F32)], axis=0)
+    for tile in range(8):
+        turned[pl.ds(tile * 128, 128), :] = small[:, tile * 128 : tile * 128 + 128].T
+
+    def scatter(i, carry):
+        eight = turned[pl.ds(pl.multiple_of(i * 8, 8), 8), :]
+        x_hi, core, x_lo = i // 64, lax.rem(i // 32, 2), lax.rem(i // 16, 2)
+        y, z = lax.rem(i // 4, 4), lax.rem(i, 4) * 2
+        grads[x_hi, core, x_lo, y, z, :, pl.ds(1536, 128)] = eight.astype(BF16)
+        grads[x_hi, core, x_lo, y, z + 1, :, pl.ds(1536, 128)] = pltpu.roll(eight, 4, 0).astype(BF16)
+        return carry
+
+    lax.fori_loop(0, 128, scatter, 0)
+    sum_phase(where, send, grads, total_out, *sum_scratch)
     for copy in started:
         copy.wait_send()
 
 
-def sum_everywhere(grads):
+def on_device(
+    residual, projections, out_weight, gain_one, up_weight, conv_kernel, gain_two, down_weight,
+    lengths, out_grad,
+):
+    context = attend(projections, lengths)
     dma = pltpu.SemaphoreType.DMA
     wide, narrow = PART_Y[1], PART_Z[1]
+    vmem_spec = pl.BlockSpec(memory_space=pltpu.VMEM)
+    any_spec = pl.BlockSpec(memory_space=pl.ANY)
 
     def vmem(*shape):
         return pltpu.VMEM(shape, BF16)
 
-    return pl.pallas_call(
-        sum_kernel,
-        out_shape=jax.ShapeDtypeStruct((8, CHUNK), F32),
-        in_specs=[pl.BlockSpec(memory_space=pl.ANY)],
-        out_specs=pl.BlockSpec(memory_space=pltpu.VMEM),
+    def wide_vmem(*shape):
+        return pltpu.VMEM(shape, F32)
+
+    block, total = pl.pallas_call(
+        block_kernel,
+        out_shape=(
+            jax.ShapeDtypeStruct((256, 1024), BF16),
+            jax.ShapeDtypeStruct((8, CHUNK), F32),
+        ),
+        in_specs=[vmem_spec] * 3
+        + [pl.BlockSpec(memory_space=pltpu.SMEM)]
+        + [vmem_spec] * 3
+        + [any_spec] * 3,
+        out_specs=(vmem_spec, vmem_spec),
         scratch_shapes=[
-            vmem(2, 2, 4, 8, 8, CHUNK), vmem(2, 2, 4, 8, 8, CHUNK),
+            vmem(1024, 1024), vmem(1024, 2048), vmem(1024, 1024),
+            wide_vmem(256, 128), wide_vmem(256, 1024), wide_vmem(256, 1024),
+            vmem(256, 1024), wide_vmem(256, 1024), wide_vmem(256, 1024), vmem(256, 1024),
+            wide_vmem(384, 1024), wide_vmem(384, 1024), wide_vmem(384, 1024),
+            wide_vmem(384, 1024), wide_vmem(256, 1024), wide_vmem(8, 128),
+            wide_vmem(8, 128), vmem(256, 1024),
+            vmem(256, 1024), wide_vmem(256, 1024), vmem(256, 1024), vmem(256, 2048),
+            vmem(2, 64, 1024), vmem(2, 64, 1024),
+            wide_vmem(31, 8, 1024), wide_vmem(2, 8, 1024), wide_vmem(1024, 128),
+            vmem(2, 2, 2, 4, 8, 8, CHUNK),
+            vmem(2, 2, 4, 8, 8, CHUNK),
             vmem(3, 2, 2, 8, 8, wide), vmem(2, 2, 8, 8, wide),
             vmem(3, 8, 8, wide), vmem(8, 8, wide), vmem(7, 8, wide),
             vmem(3, 4, 8, 8, wide), vmem(4, 8, 8, wide),
             vmem(3, 8, 8, wide), vmem(8, 8, wide), vmem(7, 8, wide),
             vmem(7, 2, 2, 4, 8, narrow), vmem(2, 2, 4, 8, narrow),
             vmem(3, 4, 8, narrow), vmem(4, 8, narrow), vmem(3, 8, narrow),
-            dma((3,)), dma((48,)), dma((48,)),
+            dma((3,)), dma((56,)), dma((56,)),
         ],
         compiler_params=pltpu.CompilerParams(
-            collective_id=2, has_side_effects=True, vmem_limit_bytes=48 << 20
+            collective_id=2, has_side_effects=True, vmem_limit_bytes=58 << 20
         ),
-        name="sum_everywhere",
-    )(grads.reshape(2, 2, 2, 4, 8, 8, CHUNK))
-
-
-def extended(x, sides, width):
-    for axis, dim in sides:
-        size, length = (lax.axis_size(axis), x.shape[dim])
-        up = [(i, (i + 1) % size) for i in range(size - 1)]
-        down = [(j, i) for i, j in up]
-        last = lax.slice_in_dim(x, length - width, length, axis=dim)
-        leading = lax.slice_in_dim(x, 0, width, axis=dim)
-        before = lax.ppermute(last, axis, up)
-        after = lax.ppermute(leading, axis, down)
-        x = jnp.concatenate([before, x, after], axis=dim)
-    return x
-
-
-def normalize(values):
-    center = values - jnp.mean(values, axis=-1, keepdims=True)
-    inverse = lax.rsqrt(jnp.mean(center * center, axis=-1, keepdims=True) + EPSILON)
-    return (center * inverse, inverse)
-
-
-def on_device(
-    residual,
-    projections,
-    out_weight,
-    gain_one,
-    up_weight,
-    conv_kernel,
-    gain_two,
-    down_weight,
-    lengths,
-    out_grad,
-):
-    frames, utter_count, model_width = residual.shape
-    kernel_len = conv_kernel.shape[0]
-    half_width = (kernel_len - 1) // 2
-    row_count = frames * utter_count
-    first_frame = lax.axis_index("ctx") * frames
-    positions = first_frame + jnp.arange(frames, dtype=jnp.int32)
-    valid = (positions[:, None] < lengths[None, :]).astype(jnp.bfloat16)
-    context = attend(projections, lengths)
-    hidden = residual.reshape(row_count, model_width).astype(jnp.float32) + jnp.dot(
-        context, out_weight, preferred_element_type=jnp.float32
+        name="block_and_sums",
+    )(
+        context,
+        residual.reshape(256, 1024),
+        out_grad.reshape(256, 1024),
+        lengths,
+        gain_one.reshape(1, 1024),
+        gain_two.reshape(1, 1024),
+        conv_kernel,
+        out_weight,
+        up_weight,
+        down_weight,
     )
-    normed_one, inverse_one = normalize(hidden)
-    scaled_one = (normed_one * gain_one).astype(jnp.bfloat16)
-    lifted = jnp.dot(scaled_one, up_weight, preferred_element_type=jnp.float32)
-    linear_part = lifted[:, :model_width]
-    gate_part = jax.nn.sigmoid(lifted[:, model_width:])
-    row_mask = valid.reshape(row_count, 1).astype(jnp.float32)
-    glu_out = (linear_part * gate_part * row_mask).astype(jnp.bfloat16)
-    glu_rimmed = extended(
-        glu_out.reshape(frames, utter_count, model_width), (("ctx", 0),), half_width
-    )
-    glu_wide = glu_rimmed.astype(jnp.float32)
-    conv_out = jnp.zeros((frames, utter_count, model_width), jnp.float32)
-    for offset in range(kernel_len):
-        conv_out = conv_out + conv_kernel[offset] * glu_wide[offset : offset + frames]
-    normed_two, inverse_two = normalize(conv_out.reshape(row_count, model_width))
-    pre_act = normed_two * gain_two
-    gate_two = jax.nn.sigmoid(pre_act)
-    activated = (pre_act * gate_two).astype(jnp.bfloat16)
-    block_out = (
-        hidden + jnp.dot(activated, down_weight, preferred_element_type=jnp.float32)
-    ).astype(jnp.bfloat16)
-    block_out = block_out.reshape(frames, utter_count, model_width)
-    cotangent = (out_grad * valid[:, :, None]).reshape(row_count, model_width)
-    down_grad = jnp.einsum("ro,ri->oi", cotangent, activated, preferred_element_type=jnp.float32)
-    act_grad = lax.dot_general(
-        cotangent, down_weight, (((1,), (1,)), ((), ())), preferred_element_type=jnp.float32
-    )
-    pre_grad = act_grad * gate_two * (1.0 + pre_act * (1.0 - gate_two))
-    gain_two_grad = jnp.sum(pre_grad * normed_two, axis=0)
-    scaled_grad = pre_grad * gain_two
-    conv_grad = inverse_two * (
-        scaled_grad
-        - jnp.mean(scaled_grad, axis=-1, keepdims=True)
-        - normed_two * jnp.mean(scaled_grad * normed_two, axis=-1, keepdims=True)
-    )
-    conv_grad = conv_grad.astype(jnp.bfloat16).reshape(frames, utter_count, model_width)
-    conv_rimmed = extended(conv_grad, (("ctx", 0),), half_width)
-    conv_wide = conv_rimmed.astype(jnp.float32)
-    conv_local = conv_wide[half_width : half_width + frames]
-    kernel_cols = []
-    glu_grad = jnp.zeros((frames, utter_count, model_width), jnp.float32)
-    for offset in range(kernel_len):
-        kernel_cols.append(jnp.sum(conv_local * glu_wide[offset : offset + frames], axis=(0, 1)))
-        start_row = 2 * half_width - offset
-        glu_grad = glu_grad + conv_kernel[offset] * conv_wide[start_row : start_row + frames]
-    glu_grad = glu_grad.reshape(row_count, model_width) * row_mask
-    linear_grad = glu_grad * gate_part
-    gate_grad = glu_grad * linear_part * gate_part * (1.0 - gate_part)
-    lifted_grad = jnp.concatenate([linear_grad, gate_grad], axis=1).astype(jnp.bfloat16)
-    up_grad = jnp.einsum("rj,ri->ji", lifted_grad, scaled_one, preferred_element_type=jnp.float32)
-    input_grad = lax.dot_general(
-        lifted_grad, up_weight, (((1,), (1,)), ((), ())), preferred_element_type=jnp.float32
-    )
-    gain_one_grad = jnp.sum(input_grad * normed_one, axis=0)
-    small = jnp.stack(kernel_cols + [gain_one_grad, gain_two_grad], axis=1).reshape(256, 4, 33)
-    chunks = jnp.concatenate(
-        [
-            up_grad.astype(BF16).reshape(256, 8, 1024),
-            down_grad.astype(BF16).reshape(256, 4, 2, 512).transpose(0, 2, 1, 3).reshape(256, 8, 512),
-            jnp.pad(small.astype(BF16), ((0, 0), (0, 4), (0, 95))),
-        ],
-        axis=2,
-    )
-    total = sum_everywhere(chunks)
     return (
-        block_out,
+        block.reshape(64, 4, 1024),
         total[:, :1024],
         total[:, 1024:1536].reshape(2, 4, 512).transpose(1, 0, 2).reshape(4, 1024),
         total[:4, 1536:1567],

time: 228 us -> 166 us (0.73)
  local copies, waits for them, and re-layouts: 48.8 us -> 13.3 us
  Pallas kernels: 117 us -> 149 us
  other arithmetic: 26.2 us -> 0 us
  matrix products: 19.7 us -> 0 us
  starting transfers between devices: 12.1 us -> 0 us
    pallas_call x1, Pallas kernels: 42.9 us -> 75.6 us  [on_device(): pl.pallas_call(block_kernel, out_shape=(jax.ShapeDtypeStruct((256, 1024),...]
    dot_general x7 -> x0, matrix products: 19.7 us -> none  [the longest x1 3.51 us: on_device(): lax.dot_general(lifted_grad, up_weight, (((1,), (1,)), ((), ())), preferr...]
    ppermute x4 -> x0, starting transfers between devices: 12.1 us -> none  [the longest x2 6.57 us: extended(): after = lax.ppermute(leading, axis, down)]
    reshape x10 -> x3, local copies, waits for them, and re-layouts: 16.3 us -> 4.97 us  [the longest x1 2.03 us: on_device(): block.reshape(64, 4, 1024)]
    reduce_sum x6 -> x0, other arithmetic: 10.3 us -> none  [the longest x1 5.52 us: normalize(): center = values - jnp.mean(values, axis=-1, keepdims=True)]
    another operation x67 -> x0, local copies, waits for them, and re-layouts: 9.77 us -> none  [on_device(): jnp.stack(kernel_cols + [gain_one_grad, gain_two_grad], axis=1)]
    concatenate x1 -> x0, other arithmetic: 6.09 us -> none  [on_device(): jnp.concatenate([up_grad.astype(BF16).reshape(256, 8, 1024), down_grad.as...]
    slice x12 -> x0, local copies, waits for them, and re-layouts: 4.88 us -> none  [the longest x2 3.11 us: on_device(): conv_out = conv_out + conv_kernel[offset] * glu_wide[offset:offset + frames]]
  transfers between devices with their start and end apart: 4 -> 0, of which waited for: 0 -> 0; matrix products, arithmetic and copies ran while one was open for 12% -> 0% of each run, Pallas kernels for 0% -> 0%
where the time goes in v2:
time: 166 us; the launch traced here: 163 us
  Pallas kernels  149 us (90%)
  local copies, waits for them, and re-layouts  13.3 us (8%)
    pallas_call x1, Pallas kernels, on_device(): pl.pallas_call(block_kernel, out_shape=(jax.ShapeDtypeStruct((256, 1024),...  75.6 us
    pallas_call x1, Pallas kernels, attend(): pl.pallas_call(attend_kernel, out_shape=jax.ShapeDtypeStruct((256, 1024),...  73.8 us

profile of v2, /device:TPU:32, one launch (start us, length us, event | category | flops | bytes accessed | tf_op | source)
XLA Modules:
  0.0 163.3 jit_solution(10572722378537737555)
XLA Ops:
  0.6 0.0 copy-start.3
  0.6 2.0 %reshape.33.residual = bf16[256,1024]{1,0:T(8,128)(2,1)} reshape(bf16[64,4,1024]{2,1,0:T(4,128)(2,1)} %param.10) | data formatting | bytes 1048576 | tf_op jit(solution)/shard_map/reshape | solution.py:711
  2.6 0.0 copy-start.1
  2.6 1.4 copy-done.1
  4.1 0.0 copy-start.2
  4.1 0.7 copy-done.2
  4.7 73.8 %exchange_attend.1.context = bf16[256,1024]{1,0:T(8,128)(2,1)S(1)} custom-call(bf16[64,4,3072]{2,1,0:T(4,128)(2,1)S(1)} %copy-done.1, s32[4]{0:T(128)S(1)} %copy-done.2), custom_call_target="tpu_custom_call" | custom-call | tf_op jit(solution)/shard_map/exchange_attend/pallas_call | solution.py:188
  78.5 0.0 copy-start
  78.5 0.8 copy-done
  79.3 0.0 copy-done.3
  79.3 0.9 reshape.34.out_grad
  80.2 75.6 %block_and_sums.1 = (bf16[256,1024]{1,0:T(8,128)(2,1)}, f32[8,1664]{1,0:T(8,128)}) custom-call(bf16[256,1024]{1,0:T(8,128)(2,1)} %copy-done, bf16[256,1024]{1,0:T(8,128)(2,1)} %reshape.33.residual, bf16[256,1024]{1,0:T(8,128)(2,1)} %reshape.34.out_grad, s32[4]{0:T(128)} %lengths.3, f32[1,1024]{1,0:T(1,128)} %bitcast.6, f32[1,1024]{1,0:T(1,128)} %bitcast.7, ...), custom_call_target="tpu_custom_call" | custom-call | tf_op jit(solution)/shard_map/block_and_sums/pallas_call | solution.py:674
  155.8 2.0 %reshape.37 = bf16[64,4,1024]{2,1,0:T(4,128)(2,1)} reshape(bf16[256,1024]{1,0:T(8,128)(2,1)} %get-tuple-element.8) | data formatting | bytes 1048576 | tf_op jit(solution)/shard_map/reshape | solution.py:722
  157.9 1.5 slice_reduce_fusion
  159.3 1.3 slice.17
  160.6 0.7 slice.16
  161.3 1.4 slice.15
  162.7 0.6 reshape.38
Async XLA Ops:
  0.6 78.7 %copy-start.3 = (bf16[64,4,1024]{2,1,0:T(4,128)(2,1)S(1)}, bf16[64,4,1024]{2,1,0:T(4,128)(2,1)}, u32[]{:S(2)}) copy-start(bf16[64,4,1024]{2,1,0:T(4,128)(2,1)} %param.19) | copy-start | bytes 1572868
  2.6 1.4 copy-start.1
  4.1 0.7 copy-start.2
  78.5 0.8 copy-start

commit v3 on v0

v3 whole, which is shorter than its diff:
```python
import functools

import jax
import jax.numpy as jnp
from jax import lax
from jax.experimental import pallas as pl
from jax.experimental.pallas import tpu as pltpu
from jax.sharding import PartitionSpec as P

EPSILON = 1e-05
LOG2E = 1.4426950408889634
MESH = pl.DeviceIdType.MESH
BF16 = jnp.bfloat16
F32 = jnp.float32

UP_PARTS = ((0, 256), (256, 512), (768, 384))
DOWN_PARTS = ((0, 128), (128, 128), (256, 256))


def lane_ids(shape):
    return lax.broadcasted_iota(jnp.int32, shape, len(shape) - 1)


def dot(a, b):
    return jnp.dot(a, b, preferred_element_type=F32)


def dot_t(a, b):
    return lax.dot_general(a, b, (((1,), (1,)), ((), ())), preferred_element_type=F32)


def t_dot(a, b):
    return lax.dot_general(a, b, (((0,), (0,)), ((), ())), preferred_element_type=F32)


def sigmoid(x):
    return 1.0 / (1.0 + jnp.exp(-x))


def moments(values):
    center = values - jnp.mean(values, axis=-1, keepdims=True)
    inverse = lax.rsqrt(jnp.mean(center * center, axis=-1, keepdims=True) + EPSILON)
    return center * inverse, inverse


def loop(count, body):
    def step(i, carry):
        body(i)
        return carry

    lax.fori_loop(0, count, step, 0)


def aligned(start, size):
    return pl.ds(pl.multiple_of(start, size), size)


class Place:
    def __init__(self):
        dp, ctx = lax.axis_index("dp"), lax.axis_index("ctx")
        self.dp, self.ctx = dp, ctx
        self.x_hi, self.core = dp // 2, lax.rem(dp, 2)
        self.x_lo, self.y, self.z = ctx // 32, lax.rem(ctx // 8, 4), lax.rem(ctx, 8)
        self.sibling = (self.x_hi * 2 + 1 - self.core, ctx)

    def x_split(self, k):
        to = lax.rem(self.x_hi * 2 + self.x_lo + k, 4)
        return to // 2, lax.rem(to, 2)

    def along_x(self, k):
        hi, lo = self.x_split(k)
        return hi * 2 + self.core, lo * 32 + self.y * 8 + self.z

    def along_y(self, k):
        return self.dp, self.x_lo * 32 + lax.rem(self.y + k, 4) * 8 + self.z

    def along_z(self, k):
        return self.dp, self.x_lo * 32 + self.y * 8 + lax.rem(self.z + k, 8)


class Mail:
    def __init__(self, ssem, rsem):
        self.ssem, self.rsem, self.used, self.sent = ssem, rsem, 0, []

    def send(self, src, dst, peer):
        copy = pltpu.make_async_remote_copy(
            src_ref=src, dst_ref=dst, send_sem=self.ssem.at[self.used],
            recv_sem=self.rsem.at[self.used], device_id=peer, device_id_type=MESH,
        )
        copy.start()
        self.used += 1
        self.sent.append(copy)
        return copy

    def reserve(self, count):
        base = self.used
        self.used += count
        return base

    def close(self):
        for copy in self.sent:
            copy.wait_send()


def receive(copies):
    for copy in copies:
        copy.wait_recv()


class Sum:
    def __init__(self, place, mail, mine, parts, scratch, out, offset):
        self.place, self.mail, self.mine, self.out, self.offset = place, mail, mine, out, offset
        self.parts = parts
        self.z_lanes, self.y_lanes, self.x_lanes = [pl.ds(a, n) for a, n in parts]
        (self.y_in, self.y_sum, self.yx_in, self.yx_sum, self.yxz_in,
         self.x_in, self.x_sum, self.xy_in, self.xy_sum, self.xyz_in,
         self.z_in, self.z_sum, self.zx_in, self.zx_sum, self.zxy_in) = scratch

    @staticmethod
    def scratch(parts):
        (_, wz), (_, wy), (_, wx) = parts
        shapes = [
            (3, 2, 2, 8, 8, wy), (2, 2, 8, 8, wy), (3, 8, 8, wy), (8, 8, wy), (7, 8, wy),
            (3, 4, 8, 8, wx), (4, 8, 8, wx), (3, 8, 8, wx), (8, 8, wx), (7, 8, wx),
            (7, 2, 2, 4, 8, wz), (2, 2, 4, 8, wz), (3, 4, 8, wz), (4, 8, wz), (3, 8, wz),
        ]
        return [pltpu.VMEM(shape, BF16) for shape in shapes]

    def first(self):
        p, mine, mail = self.place, self.mine, self.mail
        self.one_y = [
            mail.send(
                mine.at[:, :, lax.rem(p.y + k, 4), :, :, self.y_lanes],
                self.y_in.at[k - 1], p.along_y(k),
            )
            for k in (1, 2, 3)
        ]
        self.one_x = []
        for k in (1, 2, 3):
            hi, lo = p.x_split(k)
            self.one_x.append(
                mail.send(
                    mine.at[hi, lo, :, :, :, self.x_lanes], self.x_in.at[k - 1], p.along_x(k)
                )
            )
        self.one_z = [
            mail.send(
                mine.at[:, :, :, lax.rem(p.z + k, 8), :, self.z_lanes],
                self.z_in.at[k - 1], p.along_z(k),
            )
            for k in range(1, 8)
        ]

    def second(self):
        p, mine, mail = self.place, self.mine, self.mail
        receive(self.one_y)

        def y_body(i):
            a, b = i // 2, lax.rem(i, 2)
            acc = mine[a, b, p.y, :, :, self.y_lanes].astype(F32)
            for k in range(3):
                acc = acc + self.y_in[k, a, b].astype(F32)
            self.y_sum[a, b] = acc.astype(BF16)

        loop(4, y_body)
        self.two_y = []
        for k in (1, 2, 3):
            hi, lo = p.x_split(k)
            self.two_y.append(
                mail.send(self.y_sum.at[hi, lo], self.yx_in.at[k - 1], p.along_x(k))
            )
        receive(self.one_x)

        def x_body(i):
            acc = mine[p.x_hi, p.x_lo, i, :, :, self.x_lanes].astype(F32)
            for k in range(3):
                acc = acc + self.x_in[k, i].astype(F32)
            self.x_sum[i] = acc.astype(BF16)

        loop(4, x_body)
        self.two_x = [
            mail.send(self.x_sum.at[lax.rem(p.y + k, 4)], self.xy_in.at[k - 1], p.along_y(k))
            for k in (1, 2, 3)
        ]
        receive(self.one_z)

        def z_body(i):
            a, b = i // 2, lax.rem(i, 2)
            acc = mine[a, b, :, p.z, :, self.z_lanes].astype(F32)
            for k in range(7):
                acc = acc + self.z_in[k, a, b].astype(F32)
            self.z_sum[a, b] = acc.astype(BF16)

        loop(4, z_body)
        self.two_z = []
        for k in (1, 2, 3):
            hi, lo = p.x_split(k)
            self.two_z.append(
                mail.send(self.z_sum.at[hi, lo], self.zx_in.at[k - 1], p.along_x(k))
            )

    def third(self):
        p, mail = self.place, self.mail

        def add(copies, own, received, dst):
            receive(copies)
            acc = own[...].astype(F32)
            for k in range(3):
                acc = acc + received[k].astype(F32)
            dst[...] = acc.astype(BF16)

        add(self.two_y, self.y_sum.at[p.x_hi, p.x_lo], self.yx_in, self.yx_sum)
        self.three_y = [
            mail.send(self.yx_sum.at[lax.rem(p.z + k, 8)], self.yxz_in.at[k - 1], p.along_z(k))
            for k in range(1, 8)
        ]
        add(self.two_x, self.x_sum.at[p.y], self.xy_in, self.xy_sum)
        self.three_x = [
            mail.send(self.xy_sum.at[lax.rem(p.z + k, 8)], self.xyz_in.at[k - 1], p.along_z(k))
            for k in range(1, 8)
        ]
        add(self.two_z, self.z_sum.at[p.x_hi, p.x_lo], self.zx_in, self.zx_sum)
        self.three_z = [
            mail.send(self.zx_sum.at[lax.rem(p.y + k, 4)], self.zxy_in.at[k - 1], p.along_y(k))
            for k in (1, 2, 3)
        ]

    def last(self):
        p = self.place
        for copies, own, received, count, (start, width) in (
            (self.three_y, self.yx_sum.at[p.z], self.yxz_in, 7, self.parts[1]),
            (self.three_x, self.xy_sum.at[p.z], self.xyz_in, 7, self.parts[2]),
            (self.three_z, self.zx_sum.at[p.y], self.zxy_in, 3, self.parts[0]),
        ):
            receive(copies)
            acc = own[...].astype(F32)
            for k in range(count):
                acc = acc + received[k].astype(F32)
            self.out[:, pl.ds(self.offset + start, width)] = acc


def four_later(src, dst):
    def body(i):
        base = pl.multiple_of(i * 8, 8)
        dst[pl.ds(base, 8), :] = jnp.concatenate(
            [src[pl.ds(base, 8), :][4:], src[pl.ds(base + 8, 8), :][:4]], axis=0
        )

    loop(47, body)


def whole_kernel(
    projections, residual, out_grad, lengths, gain_one, gain_two, taps,
    out_w_hbm, up_w_hbm, down_w_hbm,
    block_out, total_out,
    pbuf, rbuf, gbuf, rows32, kv_send, q_send, kv_recv, q_recv, o_send, o_recv,
    queries, keys, values, running, totals, context,
    load_sem, kv_ssem, q_ssem, o_ssem, kv_rsem, q_rsem, o_rsem,
    out_w, up_w, down_w, mask, hidden, normed_one, scaled_one, linear, gate, glu,
    glu_even, glu_odd, grad_even, grad_odd, conv, activated,
    cotangent, act_grad, conv_grad, lifted_grad, before, after, tap_sums, sums, turned,
    up_grads, down_grads, up_other, down_other, wsem, ssem, rsem,
    *sum_scratch,
):
    place = Place()
    mail = Mail(ssem, rsem)
    dp, me, core = place.dp, place.ctx, place.core
    group = me // 8
    loads = []
    for i, (src, dst) in enumerate(
        (
            (projections, pbuf), (out_grad, gbuf), (down_w_hbm, down_w), (residual, rbuf),
            (out_w_hbm, out_w), (up_w_hbm, up_w),
        )
    ):
        copy = pltpu.make_async_copy(src, dst, wsem.at[i])
        copy.start()
        loads.append(copy)
    barrier = pltpu.get_barrier_semaphore()

    def greet(i):
        peer = (dp, lax.rem(me + i + 1, 64))
        pl.semaphore_signal(barrier, inc=1, device_id=peer, device_id_type=MESH)

    loop(63, greet)
    for peer in [place.sibling] + [place.along_x(k) for k in (1, 2, 3)]:
        pl.semaphore_signal(barrier, inc=1, device_id=peer, device_id_type=MESH)
    loads[0].wait()

    def widen(i):
        both = jnp.concatenate([pbuf[i * 2 + n].astype(F32) for n in range(2)], axis=0)
        for tile in range(24):
            rows32[tile, aligned(i * 8, 8), :] = both[:, tile * 128 : tile * 128 + 128]

    loop(32, widen)
    low = lane_ids((64, 128)) < 64
    low32 = lane_ids((32, 128)) < 64

    def pack(i):
        utt, duo = i // 8, lax.rem(i, 8)
        rows = pl.ds(utt, 64, stride=4)
        first, second, third = [rows32[duo * 3 + n, rows, :] for n in range(3)]
        first_t, second_t = pltpu.roll(first, 64, 1), pltpu.roll(second, 64, 1)
        kv_send[i * 2] = jnp.where(low, first_t, second_t).astype(BF16)
        kv_send[i * 2 + 1] = third.astype(BF16)
        q_send[i * 2] = jnp.where(low32, first[:32], first_t[32:]).astype(BF16)
        q_send[i * 2 + 1] = jnp.where(low32, second_t[:32], second[32:]).astype(BF16)

    loop(32, pack)
    pl.semaphore_wait(barrier, 67)

    def push(src, dst, send_sem, recv_sem, target):
        @pl.when(target != me)
        def _():
            pltpu.make_async_remote_copy(
                src_ref=src, dst_ref=dst, send_sem=send_sem, recv_sem=recv_sem,
                device_id=(dp, target), device_id_type=MESH,
            ).start()

        @pl.when(target == me)
        def _():
            pltpu.make_async_copy(src, dst, recv_sem).start()

    def nth_target(i):
        return lax.rem(group + i // 8, 8) * 8 + lax.rem(place.z + i, 8)

    def push_queries(i):
        target = nth_target(i)
        push(q_send.at[target], q_recv.at[me], q_ssem, q_rsem.at[group], target)

    def push_keys(i):
        target = nth_target(i)
        push(kv_send.at[target], kv_recv.at[me], kv_ssem, kv_rsem.at[group], target)

    loop(64, push_queries)
    loop(64, push_keys)

    row = lax.broadcasted_iota(jnp.int32, (256, 128), 0)
    utt = lax.rem(row, 4)
    limit = jnp.where(
        utt < 2,
        jnp.where(utt == 0, lengths[0], lengths[1]),
        jnp.where(utt == 2, lengths[2], lengths[3]),
    )
    mask[...] = jnp.where(me * 64 + row // 4 < limit, 1.0, 0.0)
    loads[1].wait()

    def take_cotangent(i):
        four = jnp.concatenate([gbuf[i * 4 + n].astype(F32) for n in range(4)], axis=0)
        rows = aligned(i * 16, 16)
        cotangent[rows, :] = (four * jnp.tile(mask[rows, :], (1, 8))).astype(BF16)

    loop(16, take_cotangent)
    loads[2].wait()

    def lift_back(i):
        cols = aligned(i * 256, 256)
        act_grad[:, cols] = dot_t(cotangent[...], down_w[cols, :])

    loop(4, lift_back)
    loads[3].wait()

    def take_residual(i):
        both = jnp.concatenate([rbuf[i * 2 + n].astype(F32) for n in range(2)], axis=0)
        hidden[aligned(i * 8, 8), :] = both

    loop(32, take_residual)
    loads[4].wait()
    loads[5].wait()

    def clear(i):
        rows = aligned(i * 512, 512)
        running[rows, :] = jnp.full((512, 128), -1e30, F32)
        totals[rows, :] = jnp.zeros((512, 128), F32)

    loop(8, clear)
    half = lane_ids((256, 128))

    def take_queries(i):
        src = lax.rem(group - i + 8, 8)
        eight = aligned(src * 8, 8)
        pltpu.make_async_copy(q_recv.at[eight], q_recv.at[eight], q_rsem.at[src]).wait()
        query = q_recv[eight].reshape(256, 128).astype(F32) * (0.125 * LOG2E)
        high = query.astype(BF16).astype(F32)
        rest = query - high
        one = jnp.where(half == 0, 1.0, 0.0)
        early = jnp.where(half < 64, high, pltpu.roll(rest, 64, 1))
        late = jnp.where(half < 64, pltpu.roll(high, 64, 1), rest)
        queries[aligned(src * 512, 512), :] = jnp.concatenate(
            [jnp.concatenate([early, one], axis=1), jnp.concatenate([late, one], axis=1)], axis=0
        ).astype(BF16)

    loop(8, take_queries)
    length = lengths[me // 16]

    def with_keys(i, finish):
        src = lax.rem(group - i + 8, 8)
        eight = aligned(src * 8, 8)
        pltpu.make_async_copy(kv_recv.at[eight], kv_recv.at[eight], kv_rsem.at[src]).wait()
        kv = kv_recv[eight].reshape(512, 128).astype(F32)
        lane = lane_ids((512, 128))
        frame = src * 512 + lax.broadcasted_iota(jnp.int32, (512, 128), 0)
        keys[:, :128] = jnp.where(lane < 64, kv, pltpu.roll(kv, 64, 1)).astype(BF16)
        keys[:, 128:] = jnp.where((lane == 0) & (frame >= length), -30000.0, 0.0).astype(BF16)
        values[...] = jnp.where(lane < 64, 1.0, kv).astype(BF16)

        def block_of(n):
            return aligned(lax.rem(group - n + 8, 8) * 512, 512)

        now = dot_t(queries[block_of(0), :], keys[...])
        for n in range(8):
            later = dot_t(queries[block_of(n + 1), :], keys[...]) if n < 7 else None
            rows = block_of(n)
            highest = running[rows, :]
            top = jnp.maximum(highest, jnp.max(now, axis=1, keepdims=True))
            probs = jnp.exp2(now - jnp.tile(top, (1, 4))).astype(BF16)
            total = totals[rows, :] * jnp.exp2(highest - top) + dot(probs, values[...])
            if finish is None:
                running[rows, :] = top
                totals[rows, :] = total
            else:
                finish(n, total)
            now = later

    loop(7, lambda i: with_keys(i, None))

    def reply(n, total):
        src = lax.rem(group - n + 8, 8)
        normed = total / pltpu.roll(total, 64, 1)
        result = jnp.where(half < 64, pltpu.roll(normed[:256], 64, 1), normed[256:])
        o_send[aligned(src * 8, 8)] = result.astype(BF16).reshape(8, 32, 128)

        def push_one(item):
            target = src * 8 + lax.rem(place.z + item, 8)
            push(o_send.at[target], o_recv.at[me], o_ssem, o_rsem.at[group], target)

        loop(8, push_one)

    with_keys(7, reply)

    def gather(i):
        src = lax.rem(group + i, 8)
        eight = aligned(src * 8, 8)
        pltpu.make_async_copy(o_recv.at[eight], o_recv.at[eight], o_rsem.at[src]).wait()
        for n in range(4):
            which = src * 4 + n
            utt, duo = which // 8, lax.rem(which, 8)
            left = o_recv[which * 2].astype(F32)
            right = o_recv[which * 2 + 1].astype(F32)
            upper = jnp.where(low32, left, pltpu.roll(right, 64, 1))
            lower = jnp.where(low32, pltpu.roll(left, 64, 1), right)
            rows32[duo, pl.ds(utt, 64, stride=4), :] = jnp.concatenate([upper, lower], axis=0)

    loop(8, gather)
    for tile in range(8):
        context[:, tile * 128 : tile * 128 + 128] = rows32[tile].astype(BF16)

    def project(i):
        cols = aligned(i * 256, 256)
        hidden[:, cols] = hidden[:, cols] + dot(context[...], out_w[:, cols])

    loop(4, project)

    def first_norm(i):
        rows = aligned(i * 16, 16)
        normed, _ = moments(hidden[rows, :])
        normed_one[rows, :] = normed
        scaled_one[rows, :] = (normed * gain_one[...]).astype(BF16)

    loop(16, first_norm)

    def lift(i):
        cols = aligned(i * 256, 256)
        lin = dot(scaled_one[...], up_w[:, cols])
        gated = sigmoid(dot(scaled_one[...], up_w[:, aligned(i * 256 + 1024, 256)]))
        product = (lin * gated * jnp.tile(mask[...], (1, 2))).astype(BF16)
        linear[:, cols] = lin
        gate[:, cols] = gated
        glu[:, cols] = product
        glu_even[pl.ds(64, 256), cols] = product.astype(F32)

    loop(4, lift)
    left_peer, right_peer = (dp, lax.rem(me + 63, 64)), (dp, lax.rem(me + 1, 64))

    def swap_rims(src, slot):
        return [
            mail.send(src.at[pl.ds(192, 64)], before.at[slot], right_peer),
            mail.send(src.at[pl.ds(0, 64)], after.at[slot], left_peer),
        ]

    def take_rims(copies, slot, dst):
        receive(copies)
        dst[pl.ds(0, 64), :] = jnp.where(me > 0, before[slot].astype(F32), 0.0)
        dst[pl.ds(320, 64), :] = jnp.where(me < 63, after[slot].astype(F32), 0.0)

    take_rims(swap_rims(glu, 0), 0, glu_even)
    four_later(glu_even, glu_odd)

    def tiles(body):
        def step(i):
            body(pl.multiple_of(lax.rem(i, 4) * 64, 64), aligned((i // 4) * 128, 128))

        loop(32, step)

    def shifted(even, odd, base, ahead, cols):
        if ahead % 2 == 0:
            return even[pl.ds(base + ahead * 4, 64), cols]
        return odd[pl.ds(base + ahead * 4 - 4, 64), cols]

    def convolve(base, cols):
        acc = jnp.zeros((64, 128), F32)
        for j in range(31):
            acc = acc + taps[j : j + 1, cols] * shifted(glu_even, glu_odd, base, j + 1, cols)
        conv[pl.ds(base, 64), cols] = acc

    tiles(convolve)
    sums[...] = jnp.zeros_like(sums)

    def second_norm(i):
        rows = aligned(i * 16, 16)
        normed, inverse = moments(conv[rows, :])
        pre = normed * gain_two[...]
        s = sigmoid(pre)
        activated[rows, :] = (pre * s).astype(BF16)
        back = act_grad[rows, :] * s * (1.0 + pre * (1.0 - s))
        weighted = back * normed
        sums[0] += weighted[:8] + weighted[8:]
        q = back * gain_two[...]
        mean_q = jnp.mean(q, axis=-1, keepdims=True)
        mean_qn = jnp.mean(q * normed, axis=-1, keepdims=True)
        result = (inverse * (q - mean_q - normed * mean_qn)).astype(BF16)
        conv_grad[rows, :] = result
        grad_even[pl.ds(rows.start + 64, 16), :] = result.astype(F32)

    loop(16, second_norm)
    rims = swap_rims(conv_grad, 1)

    upper = lax.broadcasted_iota(jnp.int32, (32, 8, 512), 1) < 4
    down_base = mail.reserve(2)

    def down_tile(hi, side):
        cols = aligned(hi * 512 + side * 256, 256)
        tile = t_dot(cotangent[:, cols], activated[...]).reshape(32, 8, 1024)
        first, second = tile[:, :, :512], tile[:, :, 512:]
        even = jnp.where(upper, first, pltpu.roll(second, 4, 1)).astype(BF16)
        odd = jnp.where(upper, pltpu.roll(first, 4, 1), second).astype(BF16)
        for n in range(32):
            at = (n // 16, (n // 4) % 4, 2 * (n % 4))
            down_grads[hi, side, at[0], at[1], at[2]] = even[n]
            down_grads[hi, side, at[0], at[1], at[2] + 1] = odd[n]

    def down_far(hi):
        down_tile(hi, 1 - core)
        pltpu.make_async_remote_copy(
            src_ref=down_grads.at[hi, 1 - core], dst_ref=down_other.at[hi],
            send_sem=ssem.at[down_base + hi], recv_sem=rsem.at[down_base + hi],
            device_id=place.sibling, device_id_type=MESH,
        ).start()

    loop(2, down_far)
    loop(2, lambda hi: down_tile(hi, core))

    def finish_block(i):
        cols = aligned(i * 256, 256)
        block_out[:, cols] = (hidden[:, cols] + dot(activated[...], down_w[:, cols])).astype(BF16)

    loop(4, finish_block)
    for hi in range(2):
        pltpu.make_async_copy(
            down_other.at[hi], down_other.at[hi], rsem.at[down_base + hi]
        ).wait()

    def down_join(i):
        at = (i // 8, core, lax.rem(i // 4, 2), lax.rem(i, 4))
        both = down_grads[at].astype(F32) + down_other[at[0], at[2], at[3]].astype(F32)
        down_grads[at] = both.astype(BF16)

    loop(16, down_join)
    down_sum = Sum(
        place, mail, down_grads.at[:, core], DOWN_PARTS, sum_scratch[15:], total_out, 1152
    )
    down_sum.first()

    def tap_step(i):
        cols = aligned(i * 128, 128)
        for block in range(4):
            local = grad_even[pl.ds(64 + block * 64, 64), cols]
            for j in range(31):
                product = local * shifted(glu_even, glu_odd, block * 64, j + 1, cols)
                part = jnp.sum(product.reshape(8, 8, 128), axis=0)
                if block == 0:
                    tap_sums[j, :, cols] = part
                else:
                    tap_sums[j, :, cols] += part

    loop(8, tap_step)
    take_rims(rims, 1, grad_even)
    four_later(grad_even, grad_odd)
    down_sum.second()

    def convolve_back(base, cols):
        acc = jnp.zeros((64, 128), F32)
        for j in range(31):
            acc = acc + taps[j : j + 1, cols] * shifted(grad_even, grad_odd, base, 31 - j, cols)
        rows = pl.ds(base, 64)
        g = gate[rows, cols]
        acc = acc * mask[rows, :] * g
        lifted_grad[rows, cols] = acc.astype(BF16)
        other_cols = pl.ds(pl.multiple_of(cols.start + 1024, 128), 128)
        lifted_grad[rows, other_cols] = (acc * linear[rows, cols] * (1.0 - g)).astype(BF16)

    tiles(convolve_back)
    down_sum.third()

    up_base = mail.reserve(4)
    up_lanes = pl.ds(0, 1024)

    def up_tile(i, side):
        hi, lo = i // 2, lax.rem(i, 2)
        cols = aligned(hi * 1024 + side * 512 + lo * 256, 256)
        return t_dot(lifted_grad[:, cols], scaled_one[...]).reshape(4, 8, 8, 1024)

    def up_far(i):
        hi, lo = i // 2, lax.rem(i, 2)
        up_grads[hi, 1 - core, lo, :, :, :, up_lanes] = up_tile(i, 1 - core).astype(BF16)
        pltpu.make_async_remote_copy(
            src_ref=up_grads.at[hi, 1 - core, lo, :, :, :, up_lanes],
            dst_ref=up_other.at[hi, lo, :, :, :, up_lanes],
            send_sem=ssem.at[up_base + i], recv_sem=rsem.at[up_base + i],
            device_id=place.sibling, device_id_type=MESH,
        ).start()

    loop(4, up_far)

    def input_tile(i):
        cols = aligned(i * 256, 256)
        product = dot_t(lifted_grad[...], up_w[cols, :]) * normed_one[:, cols]
        sums[1, :, cols] = jnp.sum(product.reshape(32, 8, 256), axis=0)

    loop(4, input_tile)

    rows_33 = [jnp.sum(tap_sums[j], axis=0, keepdims=True) for j in range(31)]
    rows_33 += [jnp.sum(sums[1], axis=0, keepdims=True), jnp.sum(sums[0], axis=0, keepdims=True)]
    small = jnp.concatenate(rows_33 + [jnp.zeros((128 - 33, 1024), F32)], axis=0)
    for tile in range(8):
        turned[pl.ds(tile * 128, 128), :] = small[:, tile * 128 : tile * 128 + 128].T
    small_lanes = pl.ds(1024, 128)

    def scatter(i):
        eight = turned[aligned(i * 8, 8), :]
        at = (i // 64, lax.rem(i // 32, 2), lax.rem(i // 16, 2), lax.rem(i // 4, 4))
        z = lax.rem(i, 4) * 2
        up_grads[(*at, z, slice(None), small_lanes)] = eight.astype(BF16)
        up_grads[(*at, z + 1, slice(None), small_lanes)] = pltpu.roll(eight, 4, 0).astype(BF16)

    loop(128, scatter)
    small_copy = mail.send(
        up_grads.at[:, 1 - core, :, :, :, :, small_lanes],
        up_other.at[:, :, :, :, :, small_lanes], place.sibling,
    )

    def up_near(i):
        hi, lo = i // 2, lax.rem(i, 2)
        tile = up_tile(i, core)
        arrived = up_other.at[hi, lo, :, :, :, up_lanes]
        pltpu.make_async_copy(arrived, arrived, rsem.at[up_base + i]).wait()
        up_grads[hi, core, lo, :, :, :, up_lanes] = (tile + arrived[...].astype(F32)).astype(BF16)

    loop(4, up_near)
    small_copy.wait_recv()

    def small_join(i):
        hi, lo = i // 2, lax.rem(i, 2)
        up_grads[hi, core, lo, :, :, :, small_lanes] = (
            up_grads[hi, core, lo, :, :, :, small_lanes].astype(F32)
            + up_other[hi, lo, :, :, :, small_lanes].astype(F32)
        ).astype(BF16)

    loop(4, small_join)
    up_sum = Sum(place, mail, up_grads.at[:, core], UP_PARTS, sum_scratch[:15], total_out, 0)
    up_sum.first()
    down_sum.last()
    up_sum.second()
    up_sum.third()
    up_sum.last()

    mail.close()
    for hi in range(2):
        sent = down_grads.at[hi, 1 - core]
        pltpu.make_async_copy(sent, sent, ssem.at[down_base + hi]).wait()
    for i in range(4):
        sent = up_grads.at[i // 2, 1 - core, i % 2, :, :, :, up_lanes]
        pltpu.make_async_copy(sent, sent, ssem.at[up_base + i]).wait()
    for buf, sem in ((kv_send, kv_ssem), (q_send, q_ssem), (o_send, o_ssem)):
        sent = buf.at[pl.ds(0, 63)]
        pltpu.make_async_copy(sent, sent, sem).wait()


def hand_out_kernel(block, total, block_out, up_grad, down_grad, kernel_grad, one_grad, two_grad):
    def body(i):
        eight = block[aligned(i * 16, 16), :].astype(F32)
        for n in range(4):
            block_out[i * 4 + n] = eight[n * 4 : n * 4 + 4].astype(BF16)

    loop(16, body)
    up_grad[...] = total[:, :1024]
    down = total[:, 1152:1664]
    down_grad[:, :512] = down[:4]
    down_grad[:, 512:] = down[4:]
    small = total[:, 1024:1152]
    kernel_grad[...] = small[:4, :31]
    turned = small.T
    one_grad[...] = turned[31:32, :4]
    two_grad[...] = turned[32:33, :4]


def on_device(
    residual, projections, out_weight, gain_one, up_weight, conv_kernel, gain_two, down_weight,
    lengths, out_grad,
):
    dma = pltpu.SemaphoreType.DMA
    vmem_spec = pl.BlockSpec(memory_space=pltpu.VMEM)
    any_spec = pl.BlockSpec(memory_space=pl.ANY)

    def half(*shape):
        return pltpu.VMEM(shape, BF16)

    def full(*shape):
        return pltpu.VMEM(shape, F32)

    block, total = pl.pallas_call(
        whole_kernel,
        out_shape=(
            jax.ShapeDtypeStruct((256, 1024), BF16),
            jax.ShapeDtypeStruct((8, 1664), F32),
        ),
        in_specs=[any_spec] * 3
        + [pl.BlockSpec(memory_space=pltpu.SMEM)]
        + [vmem_spec] * 3
        + [any_spec] * 3,
        out_specs=(vmem_spec, vmem_spec),
        scratch_shapes=[
            half(64, 4, 3072), half(64, 4, 1024), half(64, 4, 1024), full(24, 256, 128),
            half(64, 64, 128), half(64, 32, 128), half(64, 64, 128), half(64, 32, 128),
            half(64, 32, 128), half(64, 32, 128),
            half(4096, 256), half(512, 256), half(512, 128), full(4096, 128), full(4096, 128),
            half(256, 1024),
            dma, dma, dma, dma, dma((8,)), dma((8,)), dma((8,)),
            half(1024, 1024), half(1024, 2048), half(1024, 1024),
            full(256, 128), full(256, 1024), full(256, 1024), half(256, 1024),
            full(256, 1024), full(256, 1024), half(256, 1024),
            full(384, 1024), full(384, 1024), full(384, 1024), full(384, 1024),
            full(256, 1024), half(256, 1024),
            half(256, 1024), full(256, 1024), half(256, 1024), half(256, 2048),
            half(2, 64, 1024), half(2, 64, 1024),
            full(31, 8, 1024), full(2, 8, 1024), full(1024, 128),
            half(2, 2, 2, 4, 8, 8, 1152), half(2, 2, 2, 4, 8, 8, 512),
            half(2, 2, 4, 8, 8, 1152), half(2, 2, 4, 8, 8, 512),
            dma((6,)), dma((96,)), dma((96,)),
        ]
        + Sum.scratch(UP_PARTS)
        + Sum.scratch(DOWN_PARTS),
        compiler_params=pltpu.CompilerParams(
            collective_id=1, has_side_effects=True, vmem_limit_bytes=63 << 20
        ),
        name="whole_block",
    )(
        projections, residual, out_grad, lengths, gain_one.reshape(1, 1024),
        gain_two.reshape(1, 1024), conv_kernel, out_weight, up_weight, down_weight,
    )
    outs = pl.pallas_call(
        hand_out_kernel,
        out_shape=(
            jax.ShapeDtypeStruct((64, 4, 1024), BF16),
            jax.ShapeDtypeStruct((8, 1024), F32),
            jax.ShapeDtypeStruct((4, 1024), F32),
            jax.ShapeDtypeStruct((4, 31), F32),
            jax.ShapeDtypeStruct((1, 4), F32),
            jax.ShapeDtypeStruct((1, 4), F32),
        ),
        in_specs=[vmem_spec] * 2,
        out_specs=(vmem_spec,) * 6,
        name="hand_out",
    )(block, total)
    return (*outs[:4], outs[4].reshape(4), outs[5].reshape(4))


def solution(mesh):
    in_specs = (
        P("ctx", "dp", None),
        P("ctx", "dp", None),
        P(),
        P(),
        P(),
        P(),
        P(),
        P(),
        P("dp"),
        P("ctx", "dp", None),
    )
    out_specs = (
        P("ctx", "dp", None),
        P(("dp", "ctx"), None),
        P(("dp", "ctx"), None),
        P(("dp", "ctx"), None),
        P(("dp", "ctx")),
        P(("dp", "ctx")),
    )
    return jax.shard_map(
        on_device, mesh=mesh, in_specs=in_specs, out_specs=out_specs, check_vma=False
    )
```

time: 1860 us -> 144 us (0.08)
  waiting for transfers between devices: 1490 us -> 0 us
  Pallas kernels: 0 us -> 143 us
  blocking collectives: 83.3 us -> 0 us
  local copies, waits for them, and re-layouts: 78.8 us -> 0 us
  other arithmetic: 78 us -> 0 us
  matrix products: 66.2 us -> 0 us
  starting transfers between devices: 41.9 us -> 0 us
    reduce_scatter x1 -> x0, waiting for transfers between devices: 1280 us -> none  [on_device(): lax.psum_scatter(up_grad, ('dp', 'ctx'), scatter_dimension=0, tiled=True)]
    unnamed x3 -> x0, waiting for transfers between devices: 144 us -> none
    pallas_call x0 -> x2, Pallas kernels: none -> 143 us  [the longest x1 141 us: on_device(): pl.pallas_call(whole_kernel, out_shape=(jax.ShapeDtypeStruct((256, 1024),...]
    unnamed x1 -> x0, blocking collectives: 83.3 us -> none
    dot_general x23 -> x0, matrix products: 66.2 us -> none  [the longest x8 25 us: one_block(): jnp.einsum('mqk,kmd->qmd', weights_bf, value_rows, preferred_element_type...]
    all_to_all x3 -> x0, waiting for transfers between devices: 63.3 us -> none  [the longest x1 50.6 us: on_device(): lax.all_to_all(packed, 'ctx', split_axis=1, concat_axis=0, tiled=True)]
    reshape x15 -> x0, local copies, waits for them, and re-layouts: 31.9 us -> none  [the longest x2 8.66 us: on_device(): packed = projections.reshape(frames, ctx_count, per_device, 3 * head_size)]
    all_to_all x3 -> x0, starting transfers between devices: 29.5 us -> none  [the longest x1 12.7 us: on_device(): lax.all_to_all(key_marks, 'ctx', split_axis=1, concat_axis=0, tiled=True)]
  transfers between devices with their start and end apart: 9 -> 0, of which waited for: 5 -> 0; matrix products, arithmetic and copies ran while one was open for 4% -> 0% of each run, Pallas kernels for 0% -> 0%
where the time goes in v3:
time: 144 us
  Pallas kernels  143 us (99%)
    pallas_call x1, Pallas kernels, on_device(): pl.pallas_call(whole_kernel, out_shape=(jax.ShapeDtypeStruct((256, 1024),...  141 us

profile of v3, /device:TPU:32, one launch (start us, length us, event | category | flops | bytes accessed | tf_op | source)
XLA Modules:
  0.0 143.7 jit_solution(18218366000006015653)
XLA Ops:
  0.6 141.0 %whole_block.1 = (bf16[256,1024]{1,0:T(8,128)(2,1)}, f32[8,1664]{1,0:T(8,128)}) custom-call(bf16[64,4,3072]{2,1,0:T(4,128)(2,1)} %projections.1, bf16[64,4,1024]{2,1,0:T(4,128)(2,1)} %residual.1, bf16[64,4,1024]{2,1,0:T(4,128)(2,1)} %out_grad.1, s32[4]{0:T(128)} %lengths.1, f32[1,1024]{1,0:T(1,128)} %bitcast.4, f32[1,1024]{1,0:T(1,128)} %bitcast.5, ...), custom_call_target="tpu_custom_call" | custom-call | tf_op jit(solution)/shard_map/whole_block/pallas_call | solution.py:731
  141.7 2.0 %hand_out.1 = (bf16[64,4,1024]{2,1,0:T(4,128)(2,1)}, f32[8,1024]{1,0:T(8,128)}, f32[4,1024]{1,0:T(4,128)}, f32[4,31]{1,0:T(4,128)}, f32[1,4]{1,0:T(1,128)}, /*index=5*/f32[1,4]{1,0:T(1,128)}) custom-call(bf16[256,1024]{1,0:T(8,128)(2,1)} %get-tuple-element.14.block, f32[8,1664]{1,0:T(8,128)} %get-tuple-element.15.total), custom_call_target="tpu_custom_call" | custom-call | tf_op jit(solution)/shard_map/hand_out/pallas_call | solution.py:771

commit v4 on v3

--- a/solution.py
+++ b/solution.py
@@ -13,7 +13,8 @@
 BF16 = jnp.bfloat16
 F32 = jnp.float32
 
-UP_PARTS = ((0, 256), (256, 512), (768, 384))
+UP_PARTS = ((0, 256), (256, 384), (640, 384))
+SMALL_PARTS = ((0, 0), (0, 0), (0, 128))
 DOWN_PARTS = ((0, 128), (128, 128), (256, 256))
 
 
@@ -111,14 +112,15 @@
     def __init__(self, place, mail, mine, parts, scratch, out, offset):
         self.place, self.mail, self.mine, self.out, self.offset = place, mail, mine, out, offset
         self.parts = parts
-        self.z_lanes, self.y_lanes, self.x_lanes = [pl.ds(a, n) for a, n in parts]
+        self.one_x, self.one_y, self.one_z = [], [], []
+        self.z_lanes, self.y_lanes, self.x_lanes = [pl.ds(a, max(n, 1)) for a, n in parts]
         (self.y_in, self.y_sum, self.yx_in, self.yx_sum, self.yxz_in,
          self.x_in, self.x_sum, self.xy_in, self.xy_sum, self.xyz_in,
          self.z_in, self.z_sum, self.zx_in, self.zx_sum, self.zxy_in) = scratch
 
     @staticmethod
     def scratch(parts):
-        (_, wz), (_, wy), (_, wx) = parts
+        wz, wy, wx = [max(n, 128) for _, n in parts]
         shapes = [
             (3, 2, 2, 8, 8, wy), (2, 2, 8, 8, wy), (3, 8, 8, wy), (8, 8, wy), (7, 8, wy),
             (3, 4, 8, 8, wx), (4, 8, 8, wx), (3, 8, 8, wx), (8, 8, wx), (7, 8, wx),
@@ -126,16 +128,33 @@
         ]
         return [pltpu.VMEM(shape, BF16) for shape in shapes]
 
-    def first(self):
+    def first(self, halves=(slice(None),)):
+        self.one_x, self.one_y, self.one_z = [], [], []
+        for at in halves:
+            self.first_yz(at)
+        self.first_x()
+
+    def first_yz(self, at):
         p, mine, mail = self.place, self.mine, self.mail
-        self.one_y = [
-            mail.send(
-                mine.at[:, :, lax.rem(p.y + k, 4), :, :, self.y_lanes],
-                self.y_in.at[k - 1], p.along_y(k),
-            )
-            for k in (1, 2, 3)
-        ]
-        self.one_x = []
+        if self.parts[1][1]:
+            for k in (1, 2, 3):
+                self.one_y.append(
+                    mail.send(
+                        mine.at[at, :, lax.rem(p.y + k, 4), :, :, self.y_lanes],
+                        self.y_in.at[k - 1, at], p.along_y(k),
+                    )
+                )
+        if self.parts[0][1]:
+            for k in range(1, 8):
+                self.one_z.append(
+                    mail.send(
+                        mine.at[at, :, :, lax.rem(p.z + k, 8), :, self.z_lanes],
+                        self.z_in.at[k - 1, at], p.along_z(k),
+                    )
+                )
+
+    def first_x(self):
+        p, mine, mail = self.place, self.mine, self.mail
         for k in (1, 2, 3):
             hi, lo = p.x_split(k)
             self.one_x.append(
@@ -143,15 +162,15 @@
                     mine.at[hi, lo, :, :, :, self.x_lanes], self.x_in.at[k - 1], p.along_x(k)
                 )
             )
-        self.one_z = [
-            mail.send(
-                mine.at[:, :, :, lax.rem(p.z + k, 8), :, self.z_lanes],
-                self.z_in.at[k - 1], p.along_z(k),
-            )
-            for k in range(1, 8)
-        ]
 
     def second(self):
+        if self.parts[1][1]:
+            self.second_y()
+        self.second_x()
+        if self.parts[0][1]:
+            self.second_z()
+
+    def second_y(self):
         p, mine, mail = self.place, self.mine, self.mail
         receive(self.one_y)
 
@@ -169,6 +188,9 @@
             self.two_y.append(
                 mail.send(self.y_sum.at[hi, lo], self.yx_in.at[k - 1], p.along_x(k))
             )
+
+    def second_x(self):
+        p, mine, mail = self.place, self.mine, self.mail
         receive(self.one_x)
 
         def x_body(i):
@@ -182,6 +204,9 @@
             mail.send(self.x_sum.at[lax.rem(p.y + k, 4)], self.xy_in.at[k - 1], p.along_y(k))
             for k in (1, 2, 3)
         ]
+
+    def second_z(self):
+        p, mine, mail = self.place, self.mine, self.mail
         receive(self.one_z)
 
         def z_body(i):
@@ -209,29 +234,33 @@
                 acc = acc + received[k].astype(F32)
             dst[...] = acc.astype(BF16)
 
-        add(self.two_y, self.y_sum.at[p.x_hi, p.x_lo], self.yx_in, self.yx_sum)
-        self.three_y = [
-            mail.send(self.yx_sum.at[lax.rem(p.z + k, 8)], self.yxz_in.at[k - 1], p.along_z(k))
-            for k in range(1, 8)
-        ]
+        if self.parts[1][1]:
+            add(self.two_y, self.y_sum.at[p.x_hi, p.x_lo], self.yx_in, self.yx_sum)
+            self.three_y = [
+                mail.send(self.yx_sum.at[lax.rem(p.z + k, 8)], self.yxz_in.at[k - 1], p.along_z(k))
+                for k in range(1, 8)
+            ]
         add(self.two_x, self.x_sum.at[p.y], self.xy_in, self.xy_sum)
         self.three_x = [
             mail.send(self.xy_sum.at[lax.rem(p.z + k, 8)], self.xyz_in.at[k - 1], p.along_z(k))
             for k in range(1, 8)
         ]
-        add(self.two_z, self.z_sum.at[p.x_hi, p.x_lo], self.zx_in, self.zx_sum)
-        self.three_z = [
-            mail.send(self.zx_sum.at[lax.rem(p.y + k, 4)], self.zxy_in.at[k - 1], p.along_y(k))
-            for k in (1, 2, 3)
-        ]
+        if self.parts[0][1]:
+            add(self.two_z, self.z_sum.at[p.x_hi, p.x_lo], self.zx_in, self.zx_sum)
+            self.three_z = [
+                mail.send(self.zx_sum.at[lax.rem(p.y + k, 4)], self.zxy_in.at[k - 1], p.along_y(k))
+                for k in (1, 2, 3)
+            ]
 
     def last(self):
         p = self.place
-        for copies, own, received, count, (start, width) in (
-            (self.three_y, self.yx_sum.at[p.z], self.yxz_in, 7, self.parts[1]),
-            (self.three_x, self.xy_sum.at[p.z], self.xyz_in, 7, self.parts[2]),
-            (self.three_z, self.zx_sum.at[p.y], self.zxy_in, 3, self.parts[0]),
-        ):
+        steps = [(self.three_x, self.xy_sum.at[p.z], self.xyz_in, 7, self.parts[2])]
+        if self.parts[0][1]:
+            steps += [
+                (self.three_y, self.yx_sum.at[p.z], self.yxz_in, 7, self.parts[1]),
+                (self.three_z, self.zx_sum.at[p.y], self.zxy_in, 3, self.parts[0]),
+            ]
+        for copies, own, received, count, (start, width) in steps:
             receive(copies)
             acc = own[...].astype(F32)
             for k in range(count):
@@ -239,14 +268,14 @@
             self.out[:, pl.ds(self.offset + start, width)] = acc
 
 
-def four_later(src, dst):
+def four_later(src, dst, start, stop):
     def body(i):
-        base = pl.multiple_of(i * 8, 8)
+        base = pl.multiple_of((start + i) * 8, 8)
         dst[pl.ds(base, 8), :] = jnp.concatenate(
             [src[pl.ds(base, 8), :][4:], src[pl.ds(base + 8, 8), :][:4]], axis=0
         )
 
-    loop(47, body)
+    loop(stop - start, body)
 
 
 def whole_kernel(
@@ -259,7 +288,7 @@
     out_w, up_w, down_w, mask, hidden, normed_one, scaled_one, linear, gate, glu,
     glu_even, glu_odd, grad_even, grad_odd, conv, activated,
     cotangent, act_grad, conv_grad, lifted_grad, before, after, tap_sums, sums, turned,
-    up_grads, down_grads, up_other, down_other, wsem, ssem, rsem,
+    up_grads, down_grads, small_grads, up_other, down_other, small_other, wsem, ssem, rsem,
     *sum_scratch,
 ):
     place = Place()
@@ -493,27 +522,39 @@
         dst[pl.ds(0, 64), :] = jnp.where(me > 0, before[slot].astype(F32), 0.0)
         dst[pl.ds(320, 64), :] = jnp.where(me < 63, after[slot].astype(F32), 0.0)
 
-    take_rims(swap_rims(glu, 0), 0, glu_even)
-    four_later(glu_even, glu_odd)
-
-    def tiles(body):
+    rims = swap_rims(glu, 0)
+    four_later(glu_even, glu_odd, 8, 39)
+
+    def tiles(blocks, body):
         def step(i):
-            body(pl.multiple_of(lax.rem(i, 4) * 64, 64), aligned((i // 4) * 128, 128))
-
-        loop(32, step)
-
-    def shifted(even, odd, base, ahead, cols):
-        if ahead % 2 == 0:
-            return even[pl.ds(base + ahead * 4, 64), cols]
-        return odd[pl.ds(base + ahead * 4 - 4, 64), cols]
+            cols = aligned((i // len(blocks)) * 128, 128)
+            which = lax.rem(i, len(blocks))
+            block = blocks[0] + which * (blocks[1] - blocks[0])
+            body(pl.multiple_of(block * 64, 64), cols)
+
+        loop(8 * len(blocks), step)
+
+    def windows(even, odd, base, cols):
+        both = even[pl.ds(base, 192), cols], odd[pl.ds(base, 192), cols]
+
+        def shifted(ahead):
+            start = (ahead - ahead % 2) * 4
+            return both[ahead % 2][start : start + 64]
+
+        return shifted
 
     def convolve(base, cols):
         acc = jnp.zeros((64, 128), F32)
+        shifted = windows(glu_even, glu_odd, base, cols)
         for j in range(31):
-            acc = acc + taps[j : j + 1, cols] * shifted(glu_even, glu_odd, base, j + 1, cols)
+            acc = acc + taps[j : j + 1, cols] * shifted(j + 1)
         conv[pl.ds(base, 64), cols] = acc
 
-    tiles(convolve)
+    tiles((1, 2), convolve)
+    take_rims(rims, 0, glu_even)
+    four_later(glu_even, glu_odd, 0, 8)
+    four_later(glu_even, glu_odd, 39, 47)
+    tiles((0, 3), convolve)
     sums[...] = jnp.zeros_like(sums)
 
     def second_norm(i):
@@ -560,11 +601,6 @@
     loop(2, down_far)
     loop(2, lambda hi: down_tile(hi, core))
 
-    def finish_block(i):
-        cols = aligned(i * 256, 256)
-        block_out[:, cols] = (hidden[:, cols] + dot(activated[...], down_w[:, cols])).astype(BF16)
-
-    loop(4, finish_block)
     for hi in range(2):
         pltpu.make_async_copy(
             down_other.at[hi], down_other.at[hi], rsem.at[down_base + hi]
@@ -577,7 +613,7 @@
 
     loop(16, down_join)
     down_sum = Sum(
-        place, mail, down_grads.at[:, core], DOWN_PARTS, sum_scratch[15:], total_out, 1152
+        place, mail, down_grads.at[:, core], DOWN_PARTS, sum_scratch[15:30], total_out, 1152
     )
     down_sum.first()
 
@@ -585,8 +621,9 @@
         cols = aligned(i * 128, 128)
         for block in range(4):
             local = grad_even[pl.ds(64 + block * 64, 64), cols]
+            shifted = windows(glu_even, glu_odd, block * 64, cols)
             for j in range(31):
-                product = local * shifted(glu_even, glu_odd, block * 64, j + 1, cols)
+                product = local * shifted(j + 1)
                 part = jnp.sum(product.reshape(8, 8, 128), axis=0)
                 if block == 0:
                     tap_sums[j, :, cols] = part
@@ -595,13 +632,14 @@
 
     loop(8, tap_step)
     take_rims(rims, 1, grad_even)
-    four_later(grad_even, grad_odd)
+    four_later(grad_even, grad_odd, 0, 47)
     down_sum.second()
 
     def convolve_back(base, cols):
         acc = jnp.zeros((64, 128), F32)
+        shifted = windows(grad_even, grad_odd, base, cols)
         for j in range(31):
-            acc = acc + taps[j : j + 1, cols] * shifted(grad_even, grad_odd, base, 31 - j, cols)
+            acc = acc + taps[j : j + 1, cols] * shifted(31 - j)
         rows = pl.ds(base, 64)
         g = gate[rows, cols]
         acc = acc * mask[rows, :] * g
@@ -609,28 +647,38 @@
         other_cols = pl.ds(pl.multiple_of(cols.start + 1024, 128), 128)
         lifted_grad[rows, other_cols] = (acc * linear[rows, cols] * (1.0 - g)).astype(BF16)
 
-    tiles(convolve_back)
+    tiles((0, 1, 2, 3), convolve_back)
     down_sum.third()
 
     up_base = mail.reserve(4)
-    up_lanes = pl.ds(0, 1024)
-
-    def up_tile(i, side):
-        hi, lo = i // 2, lax.rem(i, 2)
+    up_sum = Sum(place, mail, up_grads.at[:, core], UP_PARTS, sum_scratch[:15], total_out, 0)
+
+    def up_tile(hi, lo, side):
         cols = aligned(hi * 1024 + side * 512 + lo * 256, 256)
         return t_dot(lifted_grad[:, cols], scaled_one[...]).reshape(4, 8, 8, 1024)
 
     def up_far(i):
         hi, lo = i // 2, lax.rem(i, 2)
-        up_grads[hi, 1 - core, lo, :, :, :, up_lanes] = up_tile(i, 1 - core).astype(BF16)
+        up_grads[hi, 1 - core, lo] = up_tile(hi, lo, 1 - core).astype(BF16)
         pltpu.make_async_remote_copy(
-            src_ref=up_grads.at[hi, 1 - core, lo, :, :, :, up_lanes],
-            dst_ref=up_other.at[hi, lo, :, :, :, up_lanes],
+            src_ref=up_grads.at[hi, 1 - core, lo], dst_ref=up_other.at[hi, lo],
             send_sem=ssem.at[up_base + i], recv_sem=rsem.at[up_base + i],
             device_id=place.sibling, device_id_type=MESH,
         ).start()
 
     loop(4, up_far)
+
+    for hi in range(2):
+
+        def up_near(lo):
+            tile = up_tile(hi, lo, core)
+            arrived = up_other.at[hi, lo]
+            pltpu.make_async_copy(arrived, arrived, rsem.at[up_base + hi * 2 + lo]).wait()
+            up_grads[hi, core, lo] = (tile + arrived[...].astype(F32)).astype(BF16)
+
+        loop(2, up_near)
+        up_sum.first_yz(hi)
+    up_sum.first_x()
 
     def input_tile(i):
         cols = aligned(i * 256, 256)
@@ -644,52 +692,49 @@
     small = jnp.concatenate(rows_33 + [jnp.zeros((128 - 33, 1024), F32)], axis=0)
     for tile in range(8):
         turned[pl.ds(tile * 128, 128), :] = small[:, tile * 128 : tile * 128 + 128].T
-    small_lanes = pl.ds(1024, 128)
 
     def scatter(i):
-        eight = turned[aligned(i * 8, 8), :]
-        at = (i // 64, lax.rem(i // 32, 2), lax.rem(i // 16, 2), lax.rem(i // 4, 4))
-        z = lax.rem(i, 4) * 2
-        up_grads[(*at, z, slice(None), small_lanes)] = eight.astype(BF16)
-        up_grads[(*at, z + 1, slice(None), small_lanes)] = pltpu.roll(eight, 4, 0).astype(BF16)
-
-    loop(128, scatter)
-    small_copy = mail.send(
-        up_grads.at[:, 1 - core, :, :, :, :, small_lanes],
-        up_other.at[:, :, :, :, :, small_lanes], place.sibling,
+        at = (i // 4, lax.rem(i // 2, 2), lax.rem(i, 2))
+        for n in range(16):
+            eight = turned[pl.ds(pl.multiple_of(i * 128 + n * 8, 8), 8), :]
+            y, z = n // 4, 2 * (n % 4)
+            small_grads[(*at, y, z)] = eight.astype(BF16)
+            small_grads[(*at, y, z + 1)] = pltpu.roll(eight, 4, 0).astype(BF16)
+
+    loop(8, scatter)
+    small_copy = mail.send(small_grads.at[:, 1 - core], small_other, place.sibling)
+
+    def finish_block(i):
+        cols = aligned(i * 256, 256)
+        block_out[:, cols] = (hidden[:, cols] + dot(activated[...], down_w[:, cols])).astype(BF16)
+
+    loop(4, finish_block)
+    small_copy.wait_recv()
+
+    def small_join(i):
+        at = i // 2, lax.rem(i, 2)
+        both = small_grads[at[0], core, at[1]].astype(F32) + small_other[at].astype(F32)
+        small_grads[at[0], core, at[1]] = both.astype(BF16)
+
+    loop(4, small_join)
+    small_sum = Sum(
+        place, mail, small_grads.at[:, core], SMALL_PARTS, sum_scratch[30:], total_out, 1024
     )
-
-    def up_near(i):
-        hi, lo = i // 2, lax.rem(i, 2)
-        tile = up_tile(i, core)
-        arrived = up_other.at[hi, lo, :, :, :, up_lanes]
-        pltpu.make_async_copy(arrived, arrived, rsem.at[up_base + i]).wait()
-        up_grads[hi, core, lo, :, :, :, up_lanes] = (tile + arrived[...].astype(F32)).astype(BF16)
-
-    loop(4, up_near)
-    small_copy.wait_recv()
-
-    def small_join(i):
-        hi, lo = i // 2, lax.rem(i, 2)
-        up_grads[hi, core, lo, :, :, :, small_lanes] = (
-            up_grads[hi, core, lo, :, :, :, small_lanes].astype(F32)
-            + up_other[hi, lo, :, :, :, small_lanes].astype(F32)
-        ).astype(BF16)
-
-    loop(4, small_join)
-    up_sum = Sum(place, mail, up_grads.at[:, core], UP_PARTS, sum_scratch[:15], total_out, 0)
-    up_sum.first()
+    small_sum.first()
     down_sum.last()
     up_sum.second()
+    small_sum.second()
     up_sum.third()
+    small_sum.third()
     up_sum.last()
+    small_sum.last()
 
     mail.close()
     for hi in range(2):
         sent = down_grads.at[hi, 1 - core]
         pltpu.make_async_copy(sent, sent, ssem.at[down_base + hi]).wait()
     for i in range(4):
-        sent = up_grads.at[i // 2, 1 - core, i % 2, :, :, :, up_lanes]
+        sent = up_grads.at[i // 2, 1 - core, i % 2]
         pltpu.make_async_copy(sent, sent, ssem.at[up_base + i]).wait()
     for buf, sem in ((kv_send, kv_ssem), (q_send, q_ssem), (o_send, o_ssem)):
         sent = buf.at[pl.ds(0, 63)]
@@ -754,12 +799,14 @@
             half(256, 1024), full(256, 1024), half(256, 1024), half(256, 2048),
             half(2, 64, 1024), half(2, 64, 1024),
             full(31, 8, 1024), full(2, 8, 1024), full(1024, 128),
-            half(2, 2, 2, 4, 8, 8, 1152), half(2, 2, 2, 4, 8, 8, 512),
-            half(2, 2, 4, 8, 8, 1152), half(2, 2, 4, 8, 8, 512),
-            dma((6,)), dma((96,)), dma((96,)),
+            half(2, 2, 2, 4, 8, 8, 1024), half(2, 2, 2, 4, 8, 8, 512),
+            half(2, 2, 2, 4, 8, 8, 128),
+            half(2, 2, 4, 8, 8, 1024), half(2, 2, 4, 8, 8, 512), half(2, 2, 4, 8, 8, 128),
+            dma((6,)), dma((128,)), dma((128,)),
         ]
         + Sum.scratch(UP_PARTS)
-        + Sum.scratch(DOWN_PARTS),
+        + Sum.scratch(DOWN_PARTS)
+        + Sum.scratch(SMALL_PARTS),
         compiler_params=pltpu.CompilerParams(
             collective_id=1, has_side_effects=True, vmem_limit_bytes=63 << 20
         ),

time: 144 us -> 132 us (0.917)
  Pallas kernels: 143 us -> 132 us
    pallas_call x1, Pallas kernels: 141 us -> 130 us  [on_device(): pl.pallas_call(whole_kernel, out_shape=(jax.ShapeDtypeStruct((256, 1024),...]
where the time goes in v4:
time: 132 us
  Pallas kernels  132 us (100%)
    pallas_call x1, Pallas kernels, on_device(): pl.pallas_call(whole_kernel, out_shape=(jax.ShapeDtypeStruct((256, 1024),...  130 us

profile of v4, /device:TPU:32, one launch (start us, length us, event | category | flops | bytes accessed | tf_op | source)
XLA Modules:
  0.0 132.4 jit_solution(1998925960424041250)
XLA Ops:
  0.6 129.8 %whole_block.1 = (bf16[256,1024]{1,0:T(8,128)(2,1)}, f32[8,1664]{1,0:T(8,128)}) custom-call(bf16[64,4,3072]{2,1,0:T(4,128)(2,1)} %projections.1, bf16[64,4,1024]{2,1,0:T(4,128)(2,1)} %residual.1, bf16[64,4,1024]{2,1,0:T(4,128)(2,1)} %out_grad.1, s32[4]{0:T(128)} %lengths.1, f32[1,1024]{1,0:T(1,128)} %bitcast.4, f32[1,1024]{1,0:T(1,128)} %bitcast.5, ...), custom_call_target="tpu_custom_call" | custom-call | tf_op jit(solution)/shard_map/whole_block/pallas_call | solution.py:776
  130.4 2.0 %hand_out.1 = (bf16[64,4,1024]{2,1,0:T(4,128)(2,1)}, f32[8,1024]{1,0:T(8,128)}, f32[4,1024]{1,0:T(4,128)}, f32[4,31]{1,0:T(4,128)}, f32[1,4]{1,0:T(1,128)}, /*index=5*/f32[1,4]{1,0:T(1,128)}) custom-call(bf16[256,1024]{1,0:T(8,128)(2,1)} %get-tuple-element.14.block, f32[8,1664]{1,0:T(8,128)} %get-tuple-element.15.total), custom_call_target="tpu_custom_call" | custom-call | tf_op jit(solution)/shard_map/hand_out/pallas_call | solution.py:818

commit v5 on v4

--- a/solution.py
+++ b/solution.py
@@ -325,7 +325,22 @@
     low = lane_ids((64, 128)) < 64
     low32 = lane_ids((32, 128)) < 64
 
-    def pack(i):
+    pl.semaphore_wait(barrier, 67)
+
+    def push(src, dst, send_sem, recv_sem, target):
+        @pl.when(target != me)
+        def _():
+            pltpu.make_async_remote_copy(
+                src_ref=src, dst_ref=dst, send_sem=send_sem, recv_sem=recv_sem,
+                device_id=(dp, target), device_id_type=MESH,
+            ).start()
+
+        @pl.when(target == me)
+        def _():
+            pltpu.make_async_copy(src, dst, recv_sem).start()
+
+    def pack_and_push(step):
+        i = lax.rem(group + step // 4, 8) * 4 + lax.rem(place.z // 2 + step, 4)
         utt, duo = i // 8, lax.rem(i, 8)
         rows = pl.ds(utt, 64, stride=4)
         first, second, third = [rows32[duo * 3 + n, rows, :] for n in range(3)]
@@ -334,34 +349,16 @@
         kv_send[i * 2 + 1] = third.astype(BF16)
         q_send[i * 2] = jnp.where(low32, first[:32], first_t[32:]).astype(BF16)
         q_send[i * 2 + 1] = jnp.where(low32, second_t[:32], second[32:]).astype(BF16)
-
-    loop(32, pack)
-    pl.semaphore_wait(barrier, 67)
-
-    def push(src, dst, send_sem, recv_sem, target):
-        @pl.when(target != me)
-        def _():
-            pltpu.make_async_remote_copy(
-                src_ref=src, dst_ref=dst, send_sem=send_sem, recv_sem=recv_sem,
-                device_id=(dp, target), device_id_type=MESH,
-            ).start()
-
-        @pl.when(target == me)
-        def _():
-            pltpu.make_async_copy(src, dst, recv_sem).start()
-
-    def nth_target(i):
-        return lax.rem(group + i // 8, 8) * 8 + lax.rem(place.z + i, 8)
-
-    def push_queries(i):
-        target = nth_target(i)
-        push(q_send.at[target], q_recv.at[me], q_ssem, q_rsem.at[group], target)
+        for side in range(2):
+            target = i * 2 + side
+            push(q_send.at[target], q_recv.at[me], q_ssem, q_rsem.at[group], target)
+
+    loop(32, pack_and_push)
 
     def push_keys(i):
-        target = nth_target(i)
+        target = lax.rem(group + i // 8, 8) * 8 + lax.rem(place.z + i, 8)
         push(kv_send.at[target], kv_recv.at[me], kv_ssem, kv_rsem.at[group], target)
 
-    loop(64, push_queries)
     loop(64, push_keys)
 
     row = lax.broadcasted_iota(jnp.int32, (256, 128), 0)
@@ -485,18 +482,18 @@
         context[:, tile * 128 : tile * 128 + 128] = rows32[tile].astype(BF16)
 
     def project(i):
-        cols = aligned(i * 256, 256)
+        cols = aligned(i * 512, 512)
         hidden[:, cols] = hidden[:, cols] + dot(context[...], out_w[:, cols])
 
-    loop(4, project)
+    loop(2, project)
 
     def first_norm(i):
-        rows = aligned(i * 16, 16)
+        rows = aligned(i * 32, 32)
         normed, _ = moments(hidden[rows, :])
         normed_one[rows, :] = normed
         scaled_one[rows, :] = (normed * gain_one[...]).astype(BF16)
 
-    loop(16, first_norm)
+    loop(8, first_norm)
 
     def lift(i):
         cols = aligned(i * 256, 256)
@@ -534,20 +531,13 @@
 
         loop(8 * len(blocks), step)
 
-    def windows(even, odd, base, cols):
-        both = even[pl.ds(base, 192), cols], odd[pl.ds(base, 192), cols]
-
-        def shifted(ahead):
-            start = (ahead - ahead % 2) * 4
-            return both[ahead % 2][start : start + 64]
-
-        return shifted
-
     def convolve(base, cols):
         acc = jnp.zeros((64, 128), F32)
-        shifted = windows(glu_even, glu_odd, base, cols)
-        for j in range(31):
-            acc = acc + taps[j : j + 1, cols] * shifted(j + 1)
+        for side in range(2):
+            window = (glu_even, glu_odd)[side][pl.ds(base, 192), cols]
+            for j in range(1 - side, 31, 2):
+                start = (j + 1 - side) * 4
+                acc = acc + taps[j : j + 1, cols] * window[start : start + 64]
         conv[pl.ds(base, 64), cols] = acc
 
     tiles((1, 2), convolve)
@@ -558,22 +548,22 @@
     sums[...] = jnp.zeros_like(sums)
 
     def second_norm(i):
-        rows = aligned(i * 16, 16)
+        rows = aligned(i * 32, 32)
         normed, inverse = moments(conv[rows, :])
         pre = normed * gain_two[...]
         s = sigmoid(pre)
         activated[rows, :] = (pre * s).astype(BF16)
         back = act_grad[rows, :] * s * (1.0 + pre * (1.0 - s))
         weighted = back * normed
-        sums[0] += weighted[:8] + weighted[8:]
+        sums[0] += jnp.sum(weighted.reshape(4, 8, 1024), axis=0)
         q = back * gain_two[...]
         mean_q = jnp.mean(q, axis=-1, keepdims=True)
         mean_qn = jnp.mean(q * normed, axis=-1, keepdims=True)
         result = (inverse * (q - mean_q - normed * mean_qn)).astype(BF16)
         conv_grad[rows, :] = result
-        grad_even[pl.ds(rows.start + 64, 16), :] = result.astype(F32)
-
-    loop(16, second_norm)
+        grad_even[pl.ds(rows.start + 64, 32), :] = result.astype(F32)
+
+    loop(8, second_norm)
     rims = swap_rims(conv_grad, 1)
 
     upper = lax.broadcasted_iota(jnp.int32, (32, 8, 512), 1) < 4
@@ -621,14 +611,16 @@
         cols = aligned(i * 128, 128)
         for block in range(4):
             local = grad_even[pl.ds(64 + block * 64, 64), cols]
-            shifted = windows(glu_even, glu_odd, block * 64, cols)
-            for j in range(31):
-                product = local * shifted(j + 1)
-                part = jnp.sum(product.reshape(8, 8, 128), axis=0)
-                if block == 0:
-                    tap_sums[j, :, cols] = part
-                else:
-                    tap_sums[j, :, cols] += part
+            for side in range(2):
+                window = (glu_even, glu_odd)[side][pl.ds(block * 64, 192), cols]
+                for j in range(1 - side, 31, 2):
+                    start = (j + 1 - side) * 4
+                    product = local * window[start : start + 64]
+                    part = jnp.sum(product.reshape(8, 8, 128), axis=0)
+                    if block == 0:
+                        tap_sums[j, :, cols] = part
+                    else:
+                        tap_sums[j, :, cols] += part
 
     loop(8, tap_step)
     take_rims(rims, 1, grad_even)
@@ -637,9 +629,11 @@
 
     def convolve_back(base, cols):
         acc = jnp.zeros((64, 128), F32)
-        shifted = windows(grad_even, grad_odd, base, cols)
-        for j in range(31):
-            acc = acc + taps[j : j + 1, cols] * shifted(31 - j)
+        for side in range(2):
+            window = (grad_even, grad_odd)[side][pl.ds(base, 192), cols]
+            for j in range(1 - side, 31, 2):
+                start = (31 - j - side) * 4
+                acc = acc + taps[j : j + 1, cols] * window[start : start + 64]
         rows = pl.ds(base, 64)
         g = gate[rows, cols]
         acc = acc * mask[rows, :] * g
@@ -705,10 +699,10 @@
     small_copy = mail.send(small_grads.at[:, 1 - core], small_other, place.sibling)
 
     def finish_block(i):
-        cols = aligned(i * 256, 256)
+        cols = aligned(i * 512, 512)
         block_out[:, cols] = (hidden[:, cols] + dot(activated[...], down_w[:, cols])).astype(BF16)
 
-    loop(4, finish_block)
+    loop(2, finish_block)
     small_copy.wait_recv()
 
     def small_join(i):

time: 132 us -> 129 us (0.977)
  Pallas kernels: 132 us -> 128 us
    pallas_call x1, Pallas kernels: 130 us -> 126 us  [on_device(): pl.pallas_call(whole_kernel, out_shape=(jax.ShapeDtypeStruct((256, 1024),...]
where the time goes in v5:
time: 129 us
  Pallas kernels  128 us (99%)
    pallas_call x1, Pallas kernels, on_device(): pl.pallas_call(whole_kernel, out_shape=(jax.ShapeDtypeStruct((256, 1024),...  126 us

profile of v5, /device:TPU:32, one launch (start us, length us, event | category | flops | bytes accessed | tf_op | source)
XLA Modules:
  0.0 128.5 jit_solution(15758752774033622708)
XLA Ops:
  0.6 125.9 %whole_block.1 = (bf16[256,1024]{1,0:T(8,128)(2,1)}, f32[8,1664]{1,0:T(8,128)}) custom-call(bf16[64,4,3072]{2,1,0:T(4,128)(2,1)} %projections.1, bf16[64,4,1024]{2,1,0:T(4,128)(2,1)} %residual.1, bf16[64,4,1024]{2,1,0:T(4,128)(2,1)} %out_grad.1, s32[4]{0:T(128)} %lengths.1, f32[1,1024]{1,0:T(1,128)} %bitcast.4, f32[1,1024]{1,0:T(1,128)} %bitcast.5, ...), custom_call_target="tpu_custom_call" | custom-call | tf_op jit(solution)/shard_map/whole_block/pallas_call | solution.py:770
  126.6 2.0 %hand_out.1 = (bf16[64,4,1024]{2,1,0:T(4,128)(2,1)}, f32[8,1024]{1,0:T(8,128)}, f32[4,1024]{1,0:T(4,128)}, f32[4,31]{1,0:T(4,128)}, f32[1,4]{1,0:T(1,128)}, /*index=5*/f32[1,4]{1,0:T(1,128)}) custom-call(bf16[256,1024]{1,0:T(8,128)(2,1)} %get-tuple-element.14.block, f32[8,1664]{1,0:T(8,128)} %get-tuple-element.15.total), custom_call_target="tpu_custom_call" | custom-call | tf_op jit(solution)/shard_map/hand_out/pallas_call | solution.py:812

commit v6 on v5

--- a/solution.py
+++ b/solution.py
@@ -496,16 +496,16 @@
     loop(8, first_norm)
 
     def lift(i):
-        cols = aligned(i * 256, 256)
+        cols = aligned(i * 512, 512)
         lin = dot(scaled_one[...], up_w[:, cols])
-        gated = sigmoid(dot(scaled_one[...], up_w[:, aligned(i * 256 + 1024, 256)]))
-        product = (lin * gated * jnp.tile(mask[...], (1, 2))).astype(BF16)
+        gated = sigmoid(dot(scaled_one[...], up_w[:, aligned(i * 512 + 1024, 512)]))
+        product = (lin * gated * jnp.tile(mask[...], (1, 4))).astype(BF16)
         linear[:, cols] = lin
         gate[:, cols] = gated
         glu[:, cols] = product
         glu_even[pl.ds(64, 256), cols] = product.astype(F32)
 
-    loop(4, lift)
+    loop(2, lift)
     left_peer, right_peer = (dp, lax.rem(me + 63, 64)), (dp, lax.rem(me + 1, 64))
 
     def swap_rims(src, slot):
@@ -675,11 +675,11 @@
     up_sum.first_x()
 
     def input_tile(i):
-        cols = aligned(i * 256, 256)
+        cols = aligned(i * 512, 512)
         product = dot_t(lifted_grad[...], up_w[cols, :]) * normed_one[:, cols]
-        sums[1, :, cols] = jnp.sum(product.reshape(32, 8, 256), axis=0)
-
-    loop(4, input_tile)
+        sums[1, :, cols] = jnp.sum(product.reshape(32, 8, 512), axis=0)
+
+    loop(2, input_tile)
 
     rows_33 = [jnp.sum(tap_sums[j], axis=0, keepdims=True) for j in range(31)]
     rows_33 += [jnp.sum(sums[1], axis=0, keepdims=True), jnp.sum(sums[0], axis=0, keepdims=True)]

time: 129 us -> 128 us (level)
  no operation moved by 1% of the time
where the time goes in v6:
time: 128 us
  Pallas kernels  128 us (100%)
    pallas_call x1, Pallas kernels, on_device(): pl.pallas_call(whole_kernel, out_shape=(jax.ShapeDtypeStruct((256, 1024),...  126 us

profile of v6, /device:TPU:32, one launch (start us, length us, event | category | flops | bytes accessed | tf_op | source)
XLA Modules:
  0.0 128.2 jit_solution(515716612294737678)
XLA Ops:
  0.6 125.6 %whole_block.1 = (bf16[256,1024]{1,0:T(8,128)(2,1)}, f32[8,1664]{1,0:T(8,128)}) custom-call(bf16[64,4,3072]{2,1,0:T(4,128)(2,1)} %projections.1, bf16[64,4,1024]{2,1,0:T(4,128)(2,1)} %residual.1, bf16[64,4,1024]{2,1,0:T(4,128)(2,1)} %out_grad.1, s32[4]{0:T(128)} %lengths.1, f32[1,1024]{1,0:T(1,128)} %bitcast.4, f32[1,1024]{1,0:T(1,128)} %bitcast.5, ...), custom_call_target="tpu_custom_call" | custom-call | tf_op jit(solution)/shard_map/whole_block/pallas_call | solution.py:770
  126.2 2.0 %hand_out.1 = (bf16[64,4,1024]{2,1,0:T(4,128)(2,1)}, f32[8,1024]{1,0:T(8,128)}, f32[4,1024]{1,0:T(4,128)}, f32[4,31]{1,0:T(4,128)}, f32[1,4]{1,0:T(1,128)}, /*index=5*/f32[1,4]{1,0:T(1,128)}) custom-call(bf16[256,1024]{1,0:T(8,128)(2,1)} %get-tuple-element.14.block, f32[8,1664]{1,0:T(8,128)} %get-tuple-element.15.total), custom_call_target="tpu_custom_call" | custom-call | tf_op jit(solution)/shard_map/hand_out/pallas_call | solution.py:812
